TPU v7x, 512 devices: a whole 4x8x8 slice. The times are simulated.
512 devices in a mesh: gx: 16 (over y, core), gy: 32 (over x, z).
Axes of the slice: x: 4, y: 8, z: 8, core: 2. Of those that a mesh axis runs over, the one named last changes fastest.
Arguments:
- dens_pres: float32 [2, 128, 512, 128], P(None, 'gx', 'gy'), may hold values from 0.7 to 1.3
- velocity: float32 [3, 128, 512, 128], P(None, 'gx', 'gy'), may hold values from -0.9 to 0.9
- cut_class: int32 [128, 512, 128], P('gx', 'gy'), may hold values from 0 to 3
- nbhd_cells: int32 [16, 32, 32, 64], P('gx', 'gy'), may hold values from 0 to 16383, as said below
- helper_list: int32 [16, 32, 32], P('gx', 'gy'), may hold values from 0 to 31, as said below
- live_counts: int32 [16, 32], P('gx', 'gy'), may hold values from 16 to 32, as said below
- redist_weights: float32 [16, 32, 32, 2, 64, 64], P('gx', 'gy'), may hold values from -0.2 to 0.7
Outputs:
- new_state: float32 [5, 128, 512, 128], P(None, 'gx', 'gy')
Inputs may be any that keep to these rules, and one draw needn't show every extreme that they name: `nbhd_cells`: in each grid block the 32 x 64 entries are distinct cell numbers of that block. `helper_list`: in each grid block no helper is named by more than 2 slots, and at least one helper is named by exactly 2. `live_counts`: the slots below the count are live.
All inputs are finite; a program needn't handle non-finite values.
Results may differ from a plain program's by a relative error of at most 0.0003.
Values sent between devices are 32-bit elements; how exact they have to be, the bound alone decides.
No kernel may reach another device: no remote copies, remote signals or barrier semaphores. Data moves between devices by JAX's collectives and lax.ppermute only.
A program may use at most 64 MiB of HBM per device.

v0:
```python
import jax
import jax.numpy as jnp
from jax import lax
from jax.sharding import PartitionSpec as P

GAS_GAMMA = 1.4
STEP_RATIO = 0.3


def padded_2(cells, sides, width):
    for axis, dim in sides:
        count = lax.axis_size(axis)
        head = lax.slice_in_dim(cells, 0, width, axis=dim)
        tail = lax.slice_in_dim(cells, cells.shape[dim] - width, cells.shape[dim], axis=dim)
        cells = jnp.concatenate(
            [
                lax.ppermute(tail, axis, [(i, (i + 1) % count) for i in range(count)]),
                cells,
                lax.ppermute(head, axis, [((i + 1) % count, i) for i in range(count)]),
            ],
            axis=dim,
        )
    return cells


def minmod(lower_diff, upper_diff):
    return (
        0.5
        * (jnp.sign(lower_diff) + jnp.sign(upper_diff))
        * jnp.minimum(jnp.abs(lower_diff), jnp.abs(upper_diff))
    )


def conserved(primitive):
    density = primitive[0]
    speeds = primitive[1:4]
    pressure = primitive[4]
    energy = pressure / (GAS_GAMMA - 1.0) + 0.5 * density * jnp.sum(speeds * speeds, axis=0)
    return jnp.concatenate([density[None], density[None] * speeds, energy[None]], axis=0)


def face_flux(primitive, normal):
    density = primitive[0]
    pressure = primitive[4]
    normal_speed = primitive[1 + normal]
    state = conserved(primitive)
    flux = state * normal_speed[None]
    flux = flux.at[1 + normal].add(pressure)
    flux = flux.at[4].add(pressure * normal_speed)
    sound = jnp.sqrt(GAS_GAMMA * pressure / density)
    return (state, flux, jnp.abs(normal_speed) + sound)


def rusanov(lower_state, upper_state, normal):
    cons_low, flux_low, speed_low = face_flux(lower_state, normal)
    cons_up, flux_up, speed_up = face_flux(upper_state, normal)
    wave = jnp.maximum(speed_low, speed_up)
    return 0.5 * (flux_low + flux_up) - 0.5 * wave[None] * (cons_up - cons_low)


def piece(array, start, stop, axis):
    return lax.slice_in_dim(array, start, stop, axis=axis)


def divergence(padded, normal):
    axis = normal + 1
    length = padded.shape[axis] - 4
    jumps = piece(padded, 1, length + 4, axis) - piece(padded, 0, length + 3, axis)
    slopes = minmod(piece(jumps, 0, length + 2, axis), piece(jumps, 1, length + 3, axis))
    centres = piece(padded, 1, length + 3, axis)
    lower_state = piece(centres, 0, length + 1, axis) + 0.5 * piece(slopes, 0, length + 1, axis)
    upper_state = piece(centres, 1, length + 2, axis) - 0.5 * piece(slopes, 1, length + 2, axis)
    fluxes = rusanov(lower_state, upper_state, normal)
    return piece(fluxes, 1, length + 1, axis) - piece(fluxes, 0, length, axis)


def local(dens_pres, velocity, cut_class, nbhd_cells, helper_list, live_counts, redist_weights):
    primitive = jnp.concatenate([dens_pres[0:1], velocity, dens_pres[1:2]], axis=0)
    x_padded = padded_2(primitive, (("gx", 1),), 2)
    y_padded = padded_2(primitive, (("gy", 2),), 2)
    z_padded = jnp.pad(primitive, ((0, 0), (0, 0), (0, 0), (2, 2)), mode="wrap")
    total_div = divergence(x_padded, 0) + divergence(y_padded, 1) + divergence(z_padded, 2)
    kappa = 0.25 * (1.0 + cut_class.astype(jnp.float32))
    delta = -STEP_RATIO * total_div / kappa[None]
    flat_delta = delta.reshape(5, -1)
    total_cells = flat_delta.shape[1]
    cells = nbhd_cells[0, 0]
    helpers = helper_list[0, 0]
    slots = helpers.shape[0]
    width = cells.shape[1]
    columns = lax.axis_size("gy")
    capacity = redist_weights.shape[3]
    same = helpers[None, :] == helpers[:, None]
    lower = lax.broadcasted_iota(jnp.int32, (slots, slots), 1) < lax.broadcasted_iota(
        jnp.int32, (slots, slots), 0
    )
    ranks = jnp.sum((same & lower).astype(jnp.int32), axis=1)
    position = helpers * capacity + ranks
    placing = (
        jnp.arange(columns * capacity, dtype=jnp.int32)[:, None] == position[None, :]
    ).astype(jnp.float32)
    values = flat_delta[:, cells]
    outgoing = jnp.einsum("ps,vsw->pvw", placing, values, precision=lax.Precision.HIGHEST)
    outgoing = outgoing.reshape(columns, capacity, 5, width)
    arrived = lax.all_to_all(outgoing, "gy", split_axis=0, concat_axis=0, tiled=True)
    mixed = jnp.einsum(
        "scij,scvj->scvi", redist_weights[0, 0], arrived, precision=lax.Precision.HIGHEST
    )
    returned = lax.all_to_all(mixed, "gy", split_axis=0, concat_axis=0, tiled=True)
    results = jnp.einsum(
        "ps,pvw->vsw",
        placing,
        returned.reshape(columns * capacity, 5, width),
        precision=lax.Precision.HIGHEST,
    )
    live = jnp.arange(slots, dtype=jnp.int32) < live_counts[0, 0]
    results = jnp.where(live[None, :, None], results, values).reshape(5, slots * width)
    entry_of = (
        jnp.full((total_cells,), -1, jnp.int32)
        .at[cells.reshape(-1)]
        .set(jnp.arange(slots * width, dtype=jnp.int32))
    )
    covered = entry_of >= 0
    fetched = jnp.take(results, jnp.maximum(entry_of, 0), axis=1)
    flat_delta = jnp.where(covered[None, :], fetched, flat_delta)
    return conserved(primitive) + flat_delta.reshape(delta.shape)


def solution(mesh):
    in_specs = (
        P(None, "gx", "gy", None),
        P(None, "gx", "gy", None),
        P("gx", "gy", None),
        P("gx", "gy", None, None),
        P("gx", "gy", None),
        P("gx", "gy"),
        P("gx", "gy", None, None, None, None),
    )
    out_specs = P(None, "gx", "gy", None)
    return jax.shard_map(local, mesh=mesh, in_specs=in_specs, out_specs=out_specs, check_vma=False)
```

profile of v0, /device:TPU:32, one launch (start us, length us, event | category | flops | bytes accessed | tf_op | source)
XLA Modules:
  0.0 167.2 jit_solution(7357075922893520061)
XLA Ops:
  0.0 1.7 fusion.55
  1.7 0.9 fusion.15
  2.6 0.7 fusion.52
  3.3 3.0 %collective-permute-start.1 = (f32[5,2,16,128]{3,2,1,0:T(8,128)}, f32[5,2,16,128]{3,2,1,0:T(8,128)}, u32[]{:S(2)}, u32[]{:S(2)}) collective-permute-start(f32[5,2,16,128]{3,2,1,0:T(8,128)} %get-tuple-element.183), channel_id=1, source_target_pairs={{32,0},{64,32},{96,64},{128,96},{160,128},{192,160},{224,192},{256... | collective-permute-start | bytes 245768 | tf_op jit(solution)/shard_map/ppermute | solution.py:19
  6.3 0.7 fusion.53
  6.9 4.3 %collective-permute-start.2 = (f32[5,8,2,128]{3,2,1,0:T(2,128)}, f32[5,8,2,128]{3,2,1,0:T(2,128)}, u32[]{:S(2)}, u32[]{:S(2)}) collective-permute-start(f32[5,8,2,128]{3,2,1,0:T(2,128)} %get-tuple-element.184), channel_id=1, source_target_pairs={{0,1},{1,2},{2,3},{3,4},{4,5},{5,6},{6,7},{7,8},{8,9},{9,10},{10,1... | collective-permute-start | bytes 122888 | tf_op jit(solution)/shard_map/ppermute | solution.py:17
  11.2 10.8 %collective-permute-start.3 = (f32[5,8,2,128]{3,2,1,0:T(2,128)}, f32[5,8,2,128]{3,2,1,0:T(2,128)}, u32[]{:S(2)}, u32[]{:S(2)}) collective-permute-start(f32[5,8,2,128]{3,2,1,0:T(2,128)} %get-tuple-element.185), channel_id=1, source_target_pairs={{1,0},{2,1},{3,2},{4,3},{5,4},{6,5},{7,6},{8,7},{9,8},{10,9},{11,1... | collective-permute-start | bytes 122888 | tf_op jit(solution)/shard_map/ppermute | solution.py:19
  22.0 0.2 fusion.54
  22.2 1.3 compare_select_fusion.1
  23.5 0.8 reshape_squeeze.3
  24.3 8.1 %scatter_custom_fusion = s32[16384]{0:T(1024)S(1)} fusion(s32[2048]{0:T(1024)S(1)} %bitcast.117, s32[2048]{0:T(1024)S(1)} %iota.22, s32[]{:T(128)} %constant.324.clone.1), kind=kCustom, calls=%fused_computation.143 | custom fusion | bytes 65540 | tf_op jit(solution)/shard_map/scatter | solution.py:121
  32.4 0.6 maximum_clamp_fusion
  33.0 0.6 broadcast_compare_fusion
  33.7 1.2 pad_maximum_fusion.6
  34.9 0.2 slice_subtract_fusion
  35.2 0.5 minimum_multiply_fusion
  35.6 0.5 fusion.3
  36.2 0.1 multiply_reduce_fusion
  36.3 0.9 multiply_bitcast_fusion
  37.2 0.1 fusion.7
  37.4 0.3 copy-done.8
  38.0 0.1 copy-done.3
  38.2 0.8 copy-done.2
  39.0 0.6 add_multiply_fusion
  39.6 1.4 reshape.504
  41.0 1.3 broadcast_clamp_fusion
  42.3 0.9 convert_reduce_fusion
  43.2 1.7 %multiply_subtract_fusion = f32[5,8,16,129]{3,2,1,0:T(8,128)S(1)} fusion(f32[5,8,16,129]{3,2,1,0:T(8,128)} %copy-done.2, f32[5,8,16,129]{3,2,1,0:T(8,128)S(1)} %fusion.23, f32[1,8,16,129]{3,2,1,0:T(8,128)} %copy-done.8, f32[3,8,16,129]{3,2,1,0:T(8,128)S(1)} %slice_multiply_fusion.4, f32[1,8,16,129]{3,2,1,0:T(8,128)} %copy-done.9, ...), kind=kLoop, calls=%fused_computation.21 | loop fusion | flops 743040 | bytes 1717248 | tf_op jit(solution)/shard_map/sub | solution.py:58
  45.0 0.7 multiply_add_fusion
  45.6 0.9 pad_maximum_fusion.16
  46.6 0.4 minimum_multiply_fusion.1
  46.9 1.0 fusion.5
  47.9 0.1 multiply_bitcast_fusion.1
  48.4 0.1 multiply_subtract_fusion.1
  48.5 0.9 pad_maximum_fusion.15
  49.5 0.2 minimum_multiply_fusion.2
  49.7 0.8 fusion.9
  50.6 0.1 multiply_bitcast_fusion.2
  51.0 0.1 multiply_subtract_fusion.2
  51.1 0.2 fusion.18
  51.3 4.7 %copy.22 = f32[5,8,16,128]{0,3,2,1:T(8,128)} copy(f32[5,8,16,128]{3,2,1,0:T(8,128)S(1)} %fusion.18) | data formatting | bytes 655360 | tf_op jit(solution)/shard_map/div | solution.py:84
  56.0 10.9 %gather_fusion = f32[2048,5]{1,0:T(8,128)} fusion(f32[5,16384]{0,1:T(8,128)} %bitcast.106, s32[2048]{0:T(1024)S(1)} %copy-done.16), kind=kCustom, calls=%fused_computation | custom fusion | bytes 90112 | tf_op jit(solution)/shard_map/gather | solution.py:102
  67.0 1.6 copy.30
  68.6 0.4 fusion.35
  69.0 0.8 reshape.531
  69.8 5.1 %all-to-all-start = ((f32[32,1,640]{2,1,0:T(1,128)}), f32[32,1,640]{2,1,0:T(1,128)S(1)}, u32[]{:S(2)}, u32[]{:S(2)}) async-start(f32[32,1,640]{2,1,0:T(1,128)} %reshape.531), calls=%async_computation | async-start | bytes 163840 | tf_op jit(solution)/shard_map/all_to_all | solution.py:105
  74.9 0.7 broadcast_multiply_fusion
  75.7 9.4 %all-to-all-done = f32[32,1,640]{2,1,0:T(1,128)S(1)} async-done(((f32[32,1,640]{2,1,0:T(1,128)}), f32[32,1,640]{2,1,0:T(1,128)S(1)}, u32[]{:S(2)}, u32[]{:S(2)}) %all-to-all-start) | async-done | bytes 81952 | tf_op jit(solution)/shard_map/all_to_all | solution.py:105
  85.0 0.6 broadcast.307
  85.6 0.9 reduce.24
  86.5 0.1 reshape.532
  86.7 3.4 %fusion = f32[32,2,5,64]{3,2,1,0:T(8,128)S(1)} fusion(f32[1,1,32,2,64,64]{5,4,3,2,1,0:T(8,128)S(1)} %copy-done, f32[32,2,5,64]{3,1,2,0:T(2,128)S(1)} %bitcast.109), kind=kOutput, calls=%fused_computation.3 | convolution fusion | flops 15728640 | bytes 1212416 | tf_op jit(solution)/shard_map/scij,scvj->scvi/dot_general | solution.py:106
  90.0 0.1 copy.36
  90.1 0.8 reshape.533
  90.9 3.8 %all-to-all-start.1 = ((f32[32,1,640]{2,1,0:T(1,128)}), f32[32,1,640]{2,1,0:T(1,128)S(1)}, u32[]{:S(2)}, u32[]{:S(2)}) async-start(f32[32,1,640]{2,1,0:T(1,128)} %reshape.533), calls=%async_computation.1 | async-start | bytes 163840 | tf_op jit(solution)/shard_map/all_to_all | solution.py:109
  94.8 0.6 fusion.43
  96.1 8.8 %all-to-all-done.1 = f32[32,1,640]{2,1,0:T(1,128)S(1)} async-done(((f32[32,1,640]{2,1,0:T(1,128)}), f32[32,1,640]{2,1,0:T(1,128)S(1)}, u32[]{:S(2)}, u32[]{:S(2)}) %all-to-all-start.1) | async-done | bytes 81952 | tf_op jit(solution)/shard_map/all_to_all | solution.py:109
  104.8 0.9 reduce.25
  105.7 0.1 reshape.534
  106.0 0.2 fusion.2
  106.2 0.4 copy.31
  106.6 54.4 %gather_fusion.1 = f32[16384,5]{1,0:T(8,128)} fusion(f32[5,2048]{0,1:T(8,128)S(1)} %bitcast.105, s32[16384]{0:T(1024)S(1)} %copy-done.12), kind=kCustom, calls=%fused_computation.1 | custom fusion | bytes 720896 | tf_op jit(solution)/shard_map/jit(_take)/gather | solution.py:124
  161.1 5.3 %copy.29 = f32[5,8,16,128]{3,2,1,0:T(8,128)S(1)} copy(f32[5,8,16,128]{0,3,2,1:T(8,128)} %bitcast.107) | data formatting | bytes 655360 | tf_op jit(solution)/shard_map/jit(_take)/gather | solution.py:124
  166.4 0.8 fusion.14
  (74 shorter events, 1.3 us)
Async XLA Ops:
  0.0 86.7 %copy-start = (f32[1,1,32,2,64,64]{5,4,3,2,1,0:T(8,128)S(1)}, f32[1,1,32,2,64,64]{5,4,3,2,1,0:T(8,128)}, u32[]{:S(2)}) copy-start(f32[1,1,32,2,64,64]{5,4,3,2,1,0:T(8,128)} %param.37) | copy-start | bytes 3145732
  0.0 35.6 %copy-start.1 = (f32[3,8,16,128]{3,2,1,0:T(8,128)S(1)}, f32[3,8,16,128]{3,2,1,0:T(8,128)}, u32[]{:S(2)}) copy-start(f32[3,8,16,128]{3,2,1,0:T(8,128)} %param.32) | copy-start | bytes 589828
  3.3 45.2 %collective-permute-start = (f32[5,2,16,128]{3,2,1,0:T(8,128)}, f32[5,2,16,128]{3,2,1,0:T(8,128)S(1)}, u32[]{:S(2)}, u32[]{:S(2)}) collective-permute-start(f32[5,2,16,128]{3,2,1,0:T(8,128)} %get-tuple-element.182), channel_id=1, source_target_pairs={{0,32},{32,64},{64,96},{96,128},{128,160},{160,192},{192,224},{224... | collective-permute-start | bytes 245768 | tf_op jit(solution)/shard_map/ppermute | solution.py:17
  3.3 45.2 %collective-permute-start.1 = (f32[5,2,16,128]{3,2,1,0:T(8,128)}, f32[5,2,16,128]{3,2,1,0:T(8,128)}, u32[]{:S(2)}, u32[]{:S(2)}) collective-permute-start(f32[5,2,16,128]{3,2,1,0:T(8,128)} %get-tuple-element.183), channel_id=1, source_target_pairs={{32,0},{64,32},{96,64},{128,96},{160,128},{192,160},{224,192},{256... | collective-permute-start | bytes 245768 | tf_op jit(solution)/shard_map/ppermute | solution.py:19
  6.9 38.7 %collective-permute-start.2 = (f32[5,8,2,128]{3,2,1,0:T(2,128)}, f32[5,8,2,128]{3,2,1,0:T(2,128)}, u32[]{:S(2)}, u32[]{:S(2)}) collective-permute-start(f32[5,8,2,128]{3,2,1,0:T(2,128)} %get-tuple-element.184), channel_id=1, source_target_pairs={{0,1},{1,2},{2,3},{3,4},{4,5},{5,6},{6,7},{7,8},{8,9},{9,10},{10,1... | collective-permute-start | bytes 122888 | tf_op jit(solution)/shard_map/ppermute | solution.py:17
  11.2 34.4 %collective-permute-start.3 = (f32[5,8,2,128]{3,2,1,0:T(2,128)}, f32[5,8,2,128]{3,2,1,0:T(2,128)}, u32[]{:S(2)}, u32[]{:S(2)}) collective-permute-start(f32[5,8,2,128]{3,2,1,0:T(2,128)} %get-tuple-element.185), channel_id=1, source_target_pairs={{1,0},{2,1},{3,2},{4,3},{5,4},{6,5},{7,6},{8,7},{9,8},{10,9},{11,1... | collective-permute-start | bytes 122888 | tf_op jit(solution)/shard_map/ppermute | solution.py:19
  34.9 4.1 %copy-start.19 = (s32[8,16,128]{2,1,0:T(8,128)S(1)}, s32[8,16,128]{2,1,0:T(8,128)}, u32[]{:S(2)}) copy-start(s32[8,16,128]{2,1,0:T(8,128)} %param.33) | copy-start | bytes 196612
  37.1 0.6 copy-start.8
  37.1 0.7 copy-start.9
  37.1 0.9 copy-start.6
  37.1 0.9 copy-start.7
  37.4 0.7 copy-start.3
  38.2 0.8 copy-start.2
  48.3 2.8 %copy-start.13 = (f32[8,16,128]{2,1,0:T(8,128)S(1)}, f32[8,16,128]{2,1,0:T(8,128)}, u32[]{:S(2)}) copy-start(f32[8,16,128]{2,1,0:T(8,128)} %add_multiply_fusion) | copy-start | bytes 196612
  50.7 5.3 %copy-start.16 = (s32[2048]{0:T(1024)S(1)}, s32[2048]{0:T(1024)}, u32[]{:S(2)}) copy-start(s32[2048]{0:T(1024)} %broadcast_clamp_fusion) | copy-start | bytes 24580
  50.9 24.0 %copy-start.14 = (f32[8,16,128]{2,1,0:T(8,128)S(1)}, f32[8,16,128]{2,1,0:T(8,128)}, u32[]{:S(2)}) copy-start(f32[8,16,128]{2,1,0:T(8,128)} %get-tuple-element.191) | copy-start | bytes 196612
  51.3 54.7 %copy-start.4 = (f32[5,8,16,128]{3,2,1,0:T(8,128)}, f32[5,8,16,128]{3,2,1,0:T(8,128)S(1)}, u32[]{:S(2)}) copy-start(f32[5,8,16,128]{3,2,1,0:T(8,128)S(1)} %fusion.18) | copy-start | bytes 983044
  51.3 43.5 %copy-start.11 = (f32[2,8,16,128]{3,2,1,0:T(8,128)S(1)}, f32[2,8,16,128]{3,2,1,0:T(8,128)}, u32[]{:S(2)}) copy-start(f32[2,8,16,128]{3,2,1,0:T(8,128)} %param.31) | copy-start | bytes 393220
  51.3 55.3 %copy-start.12 = (s32[16384]{0:T(1024)S(1)}, s32[16384]{0:T(1024)}, u32[]{:S(2)}) copy-start(s32[16384]{0:T(1024)} %maximum_clamp_fusion) | copy-start | bytes 196612
  69.8 15.2 %all-to-all-start = ((f32[32,1,640]{2,1,0:T(1,128)}), f32[32,1,640]{2,1,0:T(1,128)S(1)}, u32[]{:S(2)}, u32[]{:S(2)}) async-start(f32[32,1,640]{2,1,0:T(1,128)} %reshape.531), calls=%async_computation | async-start | bytes 163840 | tf_op jit(solution)/shard_map/all_to_all | solution.py:105
  90.0 76.4 %copy-start.10 = (f32[3,8,16,128]{3,2,1,0:T(8,128)S(1)}, f32[3,8,16,128]{3,2,1,0:T(8,128)}, u32[]{:S(2)}) copy-start(f32[3,8,16,128]{3,2,1,0:T(8,128)} %get-tuple-element.188) | copy-start | bytes 589828
  90.9 13.9 %all-to-all-start.1 = ((f32[32,1,640]{2,1,0:T(1,128)}), f32[32,1,640]{2,1,0:T(1,128)S(1)}, u32[]{:S(2)}, u32[]{:S(2)}) async-start(f32[32,1,640]{2,1,0:T(1,128)} %reshape.533), calls=%async_computation.1 | async-start | bytes 163840 | tf_op jit(solution)/shard_map/all_to_all | solution.py:109
  106.6 59.8 %copy-start.15 = (f32[1,8,16,128]{3,2,1,0:T(8,128)S(1)}, f32[1,8,16,128]{3,2,1,0:T(8,128)}, u32[]{:S(2)}) copy-start(f32[1,8,16,128]{3,2,1,0:T(8,128)} %fusion.43) | copy-start | bytes 196612
  106.6 59.8 %copy-start.17 = (pred[16384]{0:T(1024)(128)(4,1)S(1)}, pred[16384]{0:T(1024)(128)(4,1)}, u32[]{:S(2)}) copy-start(pred[16384]{0:T(1024)(128)(4,1)} %get-tuple-element.193) | copy-start | bytes 49156
  161.1 5.3 %copy-start.5 = (f32[5,8,16,128]{3,2,1,0:T(8,128)S(1)}, f32[5,8,16,128]{3,2,1,0:T(8,128)}, u32[]{:S(2)}) copy-start(f32[5,8,16,128]{3,2,1,0:T(8,128)} %copy-done.4) | copy-start | bytes 983044
  161.1 5.3 %copy-start.18 = (pred[16384]{0:T(1024)(128)(4,1)S(1)}, pred[16384]{0:T(1024)(128)(4,1)}, u32[]{:S(2)}) copy-start(pred[16384]{0:T(1024)(128)(4,1)} %get-tuple-element.194) | copy-start | bytes 49156
where the time goes:
time: 168 us; the launch traced here: 167 us
  local copies, waits for them, and re-layouts  94.9 us (56%)
  starting transfers between devices  27 us (16%)
  other arithmetic  21.9 us (13%)
  waiting for transfers between devices  18.1 us (11%)
  matrix products  3.94 us (2%)
    gather x2, local copies, waits for them, and re-layouts, local(): fetched = jnp.take(results, jnp.maximum(entry_of, 0), axis=1)  59.7 us
    ppermute x2, starting transfers between devices, padded_2(): lax.ppermute(head, axis, [((i + 1) % count, i) for i in range(count)])  13.7 us
    gather x2, local copies, waits for them, and re-layouts, local(): values = flat_delta[:, cells]  12.5 us
    all_to_all x1, waiting for transfers between devices, local(): lax.all_to_all(outgoing, 'gy', split_axis=0, concat_axis=0, tiled=True)  9.35 us
    all_to_all x1, waiting for transfers between devices, local(): lax.all_to_all(mixed, 'gy', split_axis=0, concat_axis=0, tiled=True)  8.77 us
    scatter x1, local copies, waits for them, and re-layouts, local(): entry_of = jnp.full((total_cells,), -1, jnp.int32).at[cells.reshape(-1)]....  8.09 us
    all_to_all x1, starting transfers between devices, local(): lax.all_to_all(outgoing, 'gy', split_axis=0, concat_axis=0, tiled=True)  5.13 us
    div x1, local copies, waits for them, and re-layouts, local(): delta = -STEP_RATIO * total_div / kappa[None]  4.7 us
  transfers between devices with their start and end apart: 6, of which 2 were waited for; matrix products, arithmetic and copies ran while one was open for 16% of the time, Pallas kernels for 0%

commit v1 on v0

v1 whole, which is shorter than its diff:
```python
import jax
import jax.numpy as jnp
from jax import lax
from jax.experimental import pallas as pl
from jax.experimental.pallas import tpu as pltpu
from jax.sharding import PartitionSpec as P

GAS_GAMMA = 1.4
STEP_RATIO = 0.3
F32 = jnp.float32
BF16 = jnp.bfloat16
VMEM_SPEC = pl.BlockSpec(memory_space=pltpu.VMEM)
SMEM_SPEC = pl.BlockSpec(memory_space=pltpu.SMEM)


def halo_kernel(dp_ref, vel_ref, xhead_ref, xtail_ref, yhead_ref, ytail_ref):
    nx, ny = dp_ref.shape[1], dp_ref.shape[2]
    for comp in range(5):
        ref, k = (vel_ref, comp - 1) if 1 <= comp <= 3 else (dp_ref, comp // 4)
        xhead_ref[comp] = ref[k, 0:2]
        xtail_ref[comp] = ref[k, nx - 2 : nx]
        for x in range(nx):
            row = (comp * nx + x) * 2
            yhead_ref[row : row + 2, :] = ref[k, x, 0:2, :]
            ytail_ref[row : row + 2, :] = ref[k, x, ny - 2 : ny, :]


def pack_halo(dens_pres, velocity):
    _, nx, ny, nz = dens_pres.shape
    xs = jax.ShapeDtypeStruct((5, 2, ny, nz), F32)
    ys = jax.ShapeDtypeStruct((5 * nx * 2, nz), F32)
    return pl.pallas_call(
        halo_kernel,
        out_shape=(xs, xs, ys, ys),
        in_specs=[VMEM_SPEC] * 2,
        out_specs=(VMEM_SPEC,) * 4,
        name="halo_pack",
    )(dens_pres, velocity)


def weight_kernel(w_ref, o_ref):
    o_ref[...] = jnp.concatenate([w_ref[:, 0], w_ref[:, 1]], axis=-1)


def pack_weights(weights):
    blocks, cap, n, _ = weights.shape
    step = 8
    return pl.pallas_call(
        weight_kernel,
        out_shape=jax.ShapeDtypeStruct((blocks, n, cap * n), F32),
        grid=(blocks // step,),
        in_specs=[pl.BlockSpec((step, cap, n, n), lambda i: (i, 0, 0, 0))],
        out_specs=pl.BlockSpec((step, n, cap * n), lambda i: (i, 0, 0)),
        name="weight_pack",
    )(weights)


def minmod(a, b):
    return jnp.maximum(jnp.minimum(a, b), 0.0) + jnp.minimum(jnp.maximum(a, b), 0.0)


def cons_of(p):
    rho, u, v, w, pr = p
    ke = u * u + v * v + w * w
    return [rho, rho * u, rho * v, rho * w, pr * (1.0 / (GAS_GAMMA - 1.0)) + 0.5 * rho * ke]


def face_parts(p, n):
    cons = cons_of(p)
    un, pr = p[1 + n], p[4]
    flux = [c * un for c in cons]
    flux[1 + n] = flux[1 + n] + pr
    flux[4] = flux[4] + pr * un
    gp = GAS_GAMMA * pr
    speed = jnp.abs(un) + gp * lax.rsqrt(gp * p[0])
    return cons, flux, speed


def rusanov2(low, up, n):
    c0, f0, s0 = face_parts(low, n)
    c1, f1, s1 = face_parts(up, n)
    wave = jnp.maximum(s0, s1)
    return [(f0[i] + f1[i]) - wave * (c1[i] - c0[i]) for i in range(5)]


def rolled_divergence(p, axis, n):
    length = p[0].shape[axis]

    def back(v):
        return pltpu.roll(v, 1, axis)

    def ahead(v):
        return pltpu.roll(v, length - 1, axis)

    low, up = [], []
    for v in p:
        d = v - back(v)
        half = 0.5 * minmod(d, ahead(d))
        low.append(v + half)
        up.append(ahead(v - half))
    flux = rusanov2(low, up, n)
    return [f - back(f) for f in flux]


def cell_parts(c):
    row = (c >> 11) * 8 + ((c >> 7) & 7)
    lane = ((c >> 10) & 1) * 128 + (c & 127)
    return row, lane


def one_hot(ids, size):
    width = ids.shape[1]
    return lax.broadcasted_iota(jnp.int32, (size, width), 0) == ids


def flux_kernel(
    rank_ref, dp_ref, vel_ref, cut_ref, xlo_ref, xhi_ref, ylo_ref, yhi_ref, cell_ref,
    base_ref, val_ref, lhs_ref, xe, ye, dl,
):
    nx = dp_ref.shape[1]
    for comp in range(5):
        ref, k = (vel_ref, comp - 1) if 1 <= comp <= 3 else (dp_ref, comp // 4)
        xe[comp, 0:2] = xlo_ref[comp]
        xe[comp, 2 : nx + 2] = ref[k]
        xe[comp, nx + 2 : nx + 4] = xhi_ref[comp]
        for x in range(nx):
            row = (comp * nx + x) * 2
            ye[comp, x, 0:2, :] = ylo_ref[row : row + 2, :]
            ye[comp, x, 2:18, :] = ref[k, x]
            ye[comp, x, 18:20, :] = yhi_ref[row : row + 2, :]
            ye[comp, x, 20:24, :] = ref[k, x, 0:4, :]

    def plane(j):
        return [xe[c, j] for c in range(5)]

    def face_x(j):
        a, b, c, d = plane(j - 1), plane(j), plane(j + 1), plane(j + 2)
        low, up = [], []
        for i in range(5):
            mid = c[i] - b[i]
            low.append(b[i] + 0.5 * minmod(b[i] - a[i], mid))
            up.append(c[i] - 0.5 * minmod(mid, d[i] - c[i]))
        return rusanov2(low, up, 0)

    def body(x, before):
        after = face_x(x + 2)
        ydiv = rolled_divergence([ye[c, x] for c in range(5)], 0, 1)
        centre = plane(x + 2)
        zdiv = rolled_divergence(centre, 1, 2)
        kappa4 = 1.0 + cut_ref[x].astype(F32)
        scale = (-2.0 * STEP_RATIO) / kappa4
        cons = cons_of(centre)
        for i in range(5):
            delta = scale * ((after[i] - before[i]) + zdiv[i] + ydiv[i][2:18])
            base_ref[i, x] = cons[i] + delta
            row = pl.multiple_of(i * 64 + x * 8, 8)
            dl[pl.ds(row, 8), 0:128] = delta[0:8]
            dl[pl.ds(row, 8), 128:256] = delta[8:16]
        return after

    lax.fori_loop(0, nx, body, face_x(1))

    whole = dl[...]
    hi = whole.astype(BF16)
    rest = whole - hi.astype(F32)
    mid = rest.astype(BF16)
    low = (rest - mid.astype(F32)).astype(BF16)
    pieces = jnp.concatenate([hi, mid, low], axis=0)
    half_id = lax.broadcasted_iota(jnp.int32, (8, 128), 1) // 64
    for q in range(8):
        row, lane = cell_parts(cell_ref[q : q + 1, :])
        lane_hot = one_hot(lane, 256).astype(F32).astype(BF16)
        got = jnp.dot(pieces, lane_hot, preferred_element_type=F32)
        got = got[0:320] + (got[320:640] + got[640:960])
        row_hot = one_hot(row, 64)
        rows = [
            jnp.sum(jnp.where(row_hot, got[v * 64 : v * 64 + 64], 0.0), axis=0, keepdims=True)
            for v in range(5)
        ]
        val = jnp.concatenate(rows + [jnp.zeros((3, 256), F32)], axis=0)
        val_ref[q] = val
        placed = []
        for t in range(4):
            part = val[:, (t // 2) * 128 : (t // 2) * 128 + 128]
            rank = rank_ref[q * 4 + t]
            moved = jnp.where(rank == t % 2, part, pltpu.roll(part, 64, 1))
            placed.append(jnp.where(half_id == rank, moved, 0.0))
        x = jnp.concatenate(placed, axis=0)
        x_hi = x.astype(BF16)
        x_lo = (x - x_hi.astype(F32)).astype(BF16)
        both = jnp.concatenate([x_hi, x_lo], axis=0)
        lhs_ref[q] = jnp.concatenate([both, both], axis=1)


def fluxes(ranks, dens_pres, velocity, cut_class, xlo, xhi, ylo, yhi, cells):
    _, nx, ny, nz = dens_pres.shape
    return pl.pallas_call(
        flux_kernel,
        out_shape=(
            jax.ShapeDtypeStruct((5, nx, ny, nz), F32),
            jax.ShapeDtypeStruct((8, 8, 256), F32),
            jax.ShapeDtypeStruct((8, 64, 256), BF16),
        ),
        in_specs=[SMEM_SPEC] + [VMEM_SPEC] * 8,
        out_specs=(VMEM_SPEC,) * 3,
        scratch_shapes=[
            pltpu.VMEM((5, nx + 4, ny, nz), F32),
            pltpu.VMEM((5, nx, 24, nz), F32),
            pltpu.VMEM((320, 256), F32),
        ],
        name="flux_gather",
    )(ranks, dens_pres, velocity, cut_class, xlo, xhi, ylo, yhi, cells)


def contract_last(a, b):
    return lax.dot_general(a, b, (((1,), (1,)), ((), ())), preferred_element_type=F32)


def mix_kernel(helper_ref, live_ref, w_ref, lhs_ref, val_ref, cell_ref, base_ref, out_ref):
    nx = base_ref.shape[1]
    live = live_ref[0]
    slot_of = lax.broadcasted_iota(jnp.int32, (8, 256), 1) // 64
    total = jnp.zeros((320, 256), F32)
    for q in range(8):
        tiles = []
        for t in range(4):
            w = w_ref[helper_ref[q * 4 + t]]
            w_hi = w.astype(BF16)
            w_lo = (w - w_hi.astype(F32)).astype(BF16)
            tiles.append(jnp.concatenate([w_hi, w_lo], axis=1))
        made = contract_last(lhs_ref[q], jnp.concatenate(tiles, axis=0))
        made = made[0:32] + made[32:64]
        mixed = made[0:8]
        for t in range(1, 4):
            mixed = jnp.where(slot_of == t, made[t * 8 : t * 8 + 8], mixed)
        diff = jnp.where(q * 4 + slot_of < live, mixed - val_ref[q], 0.0)
        d_hi = diff.astype(BF16).astype(F32)
        d_lo = diff - d_hi
        row, lane = cell_parts(cell_ref[q : q + 1, :])
        row_hot = one_hot(row, 64)
        lane_hot = one_hot(lane, 256).astype(F32).astype(BF16)
        spread = [
            jnp.concatenate(
                [jnp.where(row_hot, d[v : v + 1, :], 0.0).astype(BF16) for v in range(5)], axis=0
            )
            for d in (d_hi, d_lo)
        ]
        total = total + contract_last(spread[0], lane_hot) + contract_last(spread[1], lane_hot)
    for v in range(5):
        for x in range(nx):
            row = v * 64 + x * 8
            out_ref[v, x, 0:8, :] = base_ref[v, x, 0:8, :] + total[row : row + 8, 0:128]
            out_ref[v, x, 8:16, :] = base_ref[v, x, 8:16, :] + total[row : row + 8, 128:256]


def redistribute(helpers, live, weights, lhs, val, cells, base):
    return pl.pallas_call(
        mix_kernel,
        out_shape=jax.ShapeDtypeStruct(base.shape, F32),
        in_specs=[SMEM_SPEC] * 2 + [VMEM_SPEC] * 5,
        out_specs=VMEM_SPEC,
        name="mix_scatter",
    )(helpers, live, weights, lhs, val, cells, base)


def local(dens_pres, velocity, cut_class, nbhd_cells, helper_list, live_counts, redist_weights):
    ngx, ngy = lax.axis_size("gx"), lax.axis_size("gy")
    packed = pack_weights(redist_weights[0, 0])
    weights = lax.all_to_all(packed, "gy", split_axis=0, concat_axis=0, tiled=True)
    xhead, xtail, yhead, ytail = pack_halo(dens_pres, velocity)
    up_x = [(i, (i + 1) % ngx) for i in range(ngx)]
    up_y = [(i, (i + 1) % ngy) for i in range(ngy)]
    ylo = lax.ppermute(ytail, "gy", up_y)
    yhi = lax.ppermute(yhead, "gy", [(b, a) for a, b in up_y])
    xlo = lax.ppermute(xtail, "gx", up_x)
    xhi = lax.ppermute(xhead, "gx", [(b, a) for a, b in up_x])
    helpers = helper_list[0, 0]
    slots = helpers.shape[0]
    same = helpers[None, :] == helpers[:, None]
    below = lax.broadcasted_iota(jnp.int32, (slots, slots), 1) < lax.broadcasted_iota(
        jnp.int32, (slots, slots), 0
    )
    ranks = jnp.sum((same & below).astype(jnp.int32), axis=1)
    cells = nbhd_cells.reshape(8, 256)
    base, val, lhs = fluxes(
        ranks, dens_pres, velocity, cut_class, xlo, xhi, ylo, yhi, cells
    )
    return redistribute(helpers, live_counts[0], weights, lhs, val, cells, base)


def solution(mesh):
    in_specs = (
        P(None, "gx", "gy", None),
        P(None, "gx", "gy", None),
        P("gx", "gy", None),
        P("gx", "gy", None, None),
        P("gx", "gy", None),
        P("gx", "gy"),
        P("gx", "gy", None, None, None, None),
    )
    out_specs = P(None, "gx", "gy", None)
    return jax.shard_map(local, mesh=mesh, in_specs=in_specs, out_specs=out_specs, check_vma=False)
```

time: 168 us -> 58.1 us (0.35)
  the two profiles are of different devices: /device:TPU:32 before, /device:TPU:48 now
where the time goes in v1:
time: 58.1 us; the launch traced here: 57.7 us
  starting transfers between devices  24.1 us (41%)
  Pallas kernels  15.5 us (27%)
  waiting for transfers between devices  13.8 us (24%)
  local copies, waits for them, and re-layouts  2.92 us (5%)
  between operations  0.73 us (1%)
  other arithmetic  0.7 us (1%)
    ppermute x1, waiting for transfers between devices, local(): ylo = lax.ppermute(ytail, 'gy', up_y)  13.8 us
    all_to_all x1, starting transfers between devices, local(): lax.all_to_all(packed, 'gy', split_axis=0, concat_axis=0, tiled=True)  13.2 us
    pallas_call x1, Pallas kernels, fluxes(): pl.pallas_call(flux_kernel, out_shape=(jax.ShapeDtypeStruct((5, nx, ny, n...  5.86 us
    ppermute x1, starting transfers between devices, local(): yhi = lax.ppermute(yhead, 'gy', [(b, a) for a, b in up_y])  5.46 us
    pallas_call x1, Pallas kernels, redistribute(): pl.pallas_call(mix_kernel, out_shape=jax.ShapeDtypeStruct(base.shape, F32...  4.16 us
    pallas_call x1, Pallas kernels, pack_weights(): pl.pallas_call(weight_kernel, out_shape=jax.ShapeDtypeStruct((blocks, n,...  3.83 us
    ppermute x1, starting transfers between devices, local(): ylo = lax.ppermute(ytail, 'gy', up_y)  3.69 us
    unnamed x14, local copies, waits for them, and re-layouts  2.25 us
  transfers between devices with their start and end apart: 5, of which 1 were waited for; matrix products, arithmetic and copies ran while one was open for 2% of the time, Pallas kernels for 13%

profile of v1, /device:TPU:48, one launch (start us, length us, event | category | flops | bytes accessed | tf_op | source)
XLA Modules:
  0.0 57.7 jit_solution(16490328415869043048)
XLA Ops:
  0.0 0.0 copy-start.6
  0.0 0.0 copy-start.5
  0.0 3.8 %weight_pack.1 = f32[32,64,128]{2,1,0:T(8,128)} custom-call(f32[32,2,64,64]{3,2,1,0:T(8,128)} %bitcast.6), custom_call_target="tpu_custom_call" | custom-call | tf_op jit(solution)/shard_map/weight_pack/pallas_call | solution.py:48
  3.8 13.2 %all-to-all-start = ((f32[32,64,128]{2,1,0:T(8,128)}), f32[32,64,128]{2,1,0:T(8,128)S(1)}, u32[]{:S(2)}, u32[]{:S(2)}) async-start(f32[32,64,128]{2,1,0:T(8,128)} %weight_pack.1), calls=%async_computation | async-start | bytes 2097152 | tf_op jit(solution)/shard_map/all_to_all | solution.py:269
  17.0 1.7 %halo_pack.1 = (f32[5,2,16,128]{3,2,1,0:T(8,128)}, f32[5,2,16,128]{3,2,1,0:T(8,128)}, f32[80,128]{1,0:T(8,128)}, f32[80,128]{1,0:T(8,128)}) custom-call(f32[2,8,16,128]{3,2,1,0:T(8,128)} %dp_ref.3, f32[3,8,16,128]{3,2,1,0:T(8,128)} %vel_ref.3), custom_call_target="tpu_custom_call" | custom-call | tf_op jit(solution)/shard_map/halo_pack/pallas_call | solution.py:32
  18.7 0.0 collective-permute-start
  18.7 1.7 %collective-permute-start.1 = (f32[5,2,16,128]{3,2,1,0:T(8,128)}, f32[5,2,16,128]{3,2,1,0:T(8,128)S(1)}, u32[]{:S(2)}, u32[]{:S(2)}) collective-permute-start(f32[5,2,16,128]{3,2,1,0:T(8,128)} %get-tuple-element.13), channel_id=1, source_target_pairs={{32,0},{64,32},{96,64},{128,96},{160,128},{192,160},{224,192},{256... | collective-permute-start | bytes 245768 | tf_op jit(solution)/shard_map/ppermute | solution.py:276
  20.4 3.7 %collective-permute-start.2 = (f32[80,128]{1,0:T(8,128)}, f32[80,128]{1,0:T(8,128)S(1)}, u32[]{:S(2)}, u32[]{:S(2)}) collective-permute-start(f32[80,128]{1,0:T(8,128)} %get-tuple-element.14), channel_id=1, source_target_pairs={{0,1},{1,2},{2,3},{3,4},{4,5},{5,6},{6,7},{7,8},{8,9},{9,10},{10,1... | collective-permute-start | bytes 122888 | tf_op jit(solution)/shard_map/ppermute | solution.py:273
  24.1 5.5 %collective-permute-start.3 = (f32[80,128]{1,0:T(8,128)}, f32[80,128]{1,0:T(8,128)S(1)}, u32[]{:S(2)}, u32[]{:S(2)}) collective-permute-start(f32[80,128]{1,0:T(8,128)} %get-tuple-element.15), channel_id=1, source_target_pairs={{1,0},{2,1},{3,2},{4,3},{5,4},{6,5},{7,6},{8,7},{9,8},{10,9},{11,1... | collective-permute-start | bytes 122888 | tf_op jit(solution)/shard_map/ppermute | solution.py:274
  29.6 0.0 copy-done.6
  29.6 0.7 %convert_reduce_fusion.rank_ref = s32[32]{0:T(128)} fusion(s32[32]{0:T(128)S(1)} %bitcast.8), kind=kLoop, calls=%fused_computation | loop fusion | flops 5088 | bytes 256 | tf_op jit(solution)/shard_map/reduce_sum | solution.py:283
  31.0 0.0 copy-done.5
  31.0 0.7 %reshape.5.cell_ref = s32[8,256]{1,0:T(8,128)} reshape(s32[1,1,32,64]{3,2,1,0:T(8,128)S(1)} %copy-done.5) | data formatting | bytes 16384 | tf_op jit(solution)/shard_map/reshape | solution.py:284
  31.6 13.8 %collective-permute-done.2.ylo_ref = f32[80,128]{1,0:T(8,128)S(1)} collective-permute-done((f32[80,128]{1,0:T(8,128)}, f32[80,128]{1,0:T(8,128)S(1)}, u32[]{:S(2)}, u32[]{:S(2)}) %collective-permute-start.2) | collective-permute-done | bytes 40992 | tf_op jit(solution)/shard_map/ppermute | solution.py:273
  45.4 0.0 copy-start.3
  45.4 0.0 collective-permute-done.3.yhi_ref
  45.4 0.0 copy-start.4
  45.4 0.0 collective-permute-done.xlo_ref
  45.4 0.0 copy-start.1
  45.5 0.0 collective-permute-done.1.xhi_ref
  45.5 0.6 %copy-done.3 = f32[80,128]{1,0:T(8,128)} copy-done((f32[80,128]{1,0:T(8,128)}, f32[80,128]{1,0:T(8,128)S(1)}, u32[]{:S(2)}) %copy-start.3) | copy-done | bytes 40984
  46.1 0.0 copy-done.4
  46.1 0.0 copy-done.1
  46.1 0.0 copy-start.2
  46.1 0.6 %copy-done.2 = f32[5,2,16,128]{3,2,1,0:T(8,128)} copy-done((f32[5,2,16,128]{3,2,1,0:T(8,128)}, f32[5,2,16,128]{3,2,1,0:T(8,128)S(1)}, u32[]{:S(2)}) %copy-start.2) | copy-done | bytes 81944
  46.7 5.9 %flux_gather.1 = (f32[5,8,16,128]{3,2,1,0:T(8,128)}, f32[8,8,256]{2,1,0:T(8,128)}, bf16[8,64,256]{2,1,0:T(8,128)(2,1)}) custom-call(s32[32]{0:T(128)} %convert_reduce_fusion.rank_ref, f32[2,8,16,128]{3,2,1,0:T(8,128)} %dp_ref.3, f32[3,8,16,128]{3,2,1,0:T(8,128)} %vel_ref.3, s32[8,16,128]{2,1,0:T(8,128)} %cut_ref.1, f32[5,2,16,128]{3,2,1,0:T(8,128)} %copy-done.1, ...), custom_call_target="tpu_custom_call" | custom-call | tf_op jit(solution)/shard_map/flux_gather/pallas_call | solution.py:197
  52.6 0.0 all-to-all-done.w_ref
  52.6 0.0 copy-start
  52.6 1.0 %copy-done = f32[32,64,128]{2,1,0:T(8,128)} copy-done((f32[32,64,128]{2,1,0:T(8,128)}, f32[32,64,128]{2,1,0:T(8,128)S(1)}, u32[]{:S(2)}) %copy-start) | copy-done | bytes 1048600
  53.6 4.2 %mix_scatter.1 = f32[5,8,16,128]{3,2,1,0:T(8,128)} custom-call(s32[32]{0:T(128)} %bitcast.7, s32[1]{0:T(128)} %bitcast.5.live_ref, f32[32,64,128]{2,1,0:T(8,128)} %copy-done, bf16[8,64,256]{2,1,0:T(8,128)(2,1)} %get-tuple-element.16.lhs_ref, f32[8,8,256]{2,1,0:T(8,128)} %get-tuple-element.17.val_ref, s32[8,256]{1,0:T(8,128)} %reshape.5.cell_ref, ...), custom_call_target="tpu_custom_call" | custom-call | tf_op jit(solution)/shard_map/mix_scatter/pallas_call | solution.py:257
Async XLA Ops:
  0.0 29.6 %copy-start.6 = (s32[1,1,32]{2,1,0:T(1,128)S(1)}, s32[1,1,32]{2,1,0:T(1,128)}, u32[]{:S(2)}) copy-start(s32[1,1,32]{2,1,0:T(1,128)} %param.11) | copy-start | bytes 388
  0.0 31.0 %copy-start.5 = (s32[1,1,32,64]{3,2,1,0:T(8,128)S(1)}, s32[1,1,32,64]{3,2,1,0:T(8,128)}, u32[]{:S(2)}) copy-start(s32[1,1,32,64]{3,2,1,0:T(8,128)} %param.10) | copy-start | bytes 24580
  3.8 48.8 %all-to-all-start = ((f32[32,64,128]{2,1,0:T(8,128)}), f32[32,64,128]{2,1,0:T(8,128)S(1)}, u32[]{:S(2)}, u32[]{:S(2)}) async-start(f32[32,64,128]{2,1,0:T(8,128)} %weight_pack.1), calls=%async_computation | async-start | bytes 2097152 | tf_op jit(solution)/shard_map/all_to_all | solution.py:269
  18.7 26.7 %collective-permute-start = (f32[5,2,16,128]{3,2,1,0:T(8,128)}, f32[5,2,16,128]{3,2,1,0:T(8,128)S(1)}, u32[]{:S(2)}, u32[]{:S(2)}) collective-permute-start(f32[5,2,16,128]{3,2,1,0:T(8,128)} %get-tuple-element.12), channel_id=1, source_target_pairs={{0,32},{32,64},{64,96},{96,128},{128,160},{160,192},{192,224},{224... | collective-permute-start | bytes 245768 | tf_op jit(solution)/shard_map/ppermute | solution.py:275
  18.7 26.8 %collective-permute-start.1 = (f32[5,2,16,128]{3,2,1,0:T(8,128)}, f32[5,2,16,128]{3,2,1,0:T(8,128)S(1)}, u32[]{:S(2)}, u32[]{:S(2)}) collective-permute-start(f32[5,2,16,128]{3,2,1,0:T(8,128)} %get-tuple-element.13), channel_id=1, source_target_pairs={{32,0},{64,32},{96,64},{128,96},{160,128},{192,160},{224,192},{256... | collective-permute-start | bytes 245768 | tf_op jit(solution)/shard_map/ppermute | solution.py:276
  20.4 25.0 %collective-permute-start.2 = (f32[80,128]{1,0:T(8,128)}, f32[80,128]{1,0:T(8,128)S(1)}, u32[]{:S(2)}, u32[]{:S(2)}) collective-permute-start(f32[80,128]{1,0:T(8,128)} %get-tuple-element.14), channel_id=1, source_target_pairs={{0,1},{1,2},{2,3},{3,4},{4,5},{5,6},{6,7},{7,8},{8,9},{9,10},{10,1... | collective-permute-start | bytes 122888 | tf_op jit(solution)/shard_map/ppermute | solution.py:273
  24.1 21.3 %collective-permute-start.3 = (f32[80,128]{1,0:T(8,128)}, f32[80,128]{1,0:T(8,128)S(1)}, u32[]{:S(2)}, u32[]{:S(2)}) collective-permute-start(f32[80,128]{1,0:T(8,128)} %get-tuple-element.15), channel_id=1, source_target_pairs={{1,0},{2,1},{3,2},{4,3},{5,4},{6,5},{7,6},{8,7},{9,8},{10,9},{11,1... | collective-permute-start | bytes 122888 | tf_op jit(solution)/shard_map/ppermute | solution.py:274
  45.4 0.6 %copy-start.3 = (f32[80,128]{1,0:T(8,128)}, f32[80,128]{1,0:T(8,128)S(1)}, u32[]{:S(2)}) copy-start(f32[80,128]{1,0:T(8,128)S(1)} %collective-permute-done.2.ylo_ref) | copy-start | bytes 122884
  45.4 0.6 %copy-start.4 = (f32[80,128]{1,0:T(8,128)}, f32[80,128]{1,0:T(8,128)S(1)}, u32[]{:S(2)}) copy-start(f32[80,128]{1,0:T(8,128)S(1)} %collective-permute-done.3.yhi_ref) | copy-start | bytes 122884
  45.4 0.7 %copy-start.1 = (f32[5,2,16,128]{3,2,1,0:T(8,128)}, f32[5,2,16,128]{3,2,1,0:T(8,128)S(1)}, u32[]{:S(2)}) copy-start(f32[5,2,16,128]{3,2,1,0:T(8,128)S(1)} %collective-permute-done.xlo_ref) | copy-start | bytes 245764
  46.1 0.6 %copy-start.2 = (f32[5,2,16,128]{3,2,1,0:T(8,128)}, f32[5,2,16,128]{3,2,1,0:T(8,128)S(1)}, u32[]{:S(2)}) copy-start(f32[5,2,16,128]{3,2,1,0:T(8,128)S(1)} %collective-permute-done.1.xhi_ref) | copy-start | bytes 245764
  52.6 1.0 %copy-start = (f32[32,64,128]{2,1,0:T(8,128)}, f32[32,64,128]{2,1,0:T(8,128)S(1)}, u32[]{:S(2)}) copy-start(f32[32,64,128]{2,1,0:T(8,128)S(1)} %all-to-all-done.w_ref) | copy-start | bytes 3145732

commit v2 on v1

v2 whole, which is shorter than its diff:
```python
import jax
import jax.numpy as jnp
from jax import lax
from jax.experimental import pallas as pl
from jax.experimental.pallas import tpu as pltpu
from jax.sharding import PartitionSpec as P

GAS_GAMMA = 1.4
STEP_RATIO = 0.3
F32 = jnp.float32
BF16 = jnp.bfloat16
VMEM_SPEC = pl.BlockSpec(memory_space=pltpu.VMEM)
SMEM_SPEC = pl.BlockSpec(memory_space=pltpu.SMEM)
ANY_SPEC = pl.BlockSpec(memory_space=pl.ANY)
PARAMS = pltpu.CompilerParams(vmem_limit_bytes=16 << 20)


def comp_ref(dp_ref, vel_ref, comp):
    return (vel_ref, comp - 1) if 1 <= comp <= 3 else (dp_ref, comp // 4)


def halo_kernel(dp_ref, vel_ref, xhead_ref, xtail_ref, yhead_ref, ytail_ref):
    for comp in range(5):
        ref, k = comp_ref(dp_ref, vel_ref, comp)
        xhead_ref[comp] = ref[k, 0:32, :]
        xtail_ref[comp] = ref[k, 96:128, :]
        for j in range(2):
            row = comp * 16 + j * 8
            yhead_ref[row : row + 8, :] = ref[k, pl.ds(j, 8, stride=16), :]
            ytail_ref[row : row + 8, :] = ref[k, pl.ds(14 + j, 8, stride=16), :]


def pack_halo(dens_pres, velocity):
    xs = jax.ShapeDtypeStruct((5, 32, 128), F32)
    ys = jax.ShapeDtypeStruct((80, 128), F32)
    return pl.pallas_call(
        halo_kernel,
        out_shape=(xs, xs, ys, ys),
        in_specs=[VMEM_SPEC] * 2,
        out_specs=(VMEM_SPEC,) * 4,
        compiler_params=PARAMS,
        name="halo_pack",
    )(dens_pres, velocity)


def weight_kernel(w_ref, o_ref, held, packed, in_sems, out_sems):
    chunks = in_sems.shape[0]
    step = w_ref.shape[0] // chunks

    def part(c):
        return pl.ds(c * step, step)

    def load(c):
        return pltpu.make_async_copy(w_ref.at[part(c)], held.at[part(c)], in_sems.at[c])

    def store(c):
        return pltpu.make_async_copy(packed.at[part(c)], o_ref.at[part(c)], out_sems.at[c])

    for c in range(chunks):
        load(c).start()
    for c in range(chunks):
        load(c).wait()
        packed[part(c)] = jnp.concatenate([held[part(c), 0], held[part(c), 1]], axis=-1)
        store(c).start()
    for c in range(chunks):
        store(c).wait()


def pack_weights(weights):
    blocks, cap, n, _ = weights.shape
    return pl.pallas_call(
        weight_kernel,
        out_shape=jax.ShapeDtypeStruct((blocks, n, cap * n), F32),
        in_specs=[ANY_SPEC],
        out_specs=ANY_SPEC,
        scratch_shapes=[
            pltpu.VMEM(weights.shape, F32),
            pltpu.VMEM((blocks, n, cap * n), F32),
            pltpu.SemaphoreType.DMA((8,)),
            pltpu.SemaphoreType.DMA((8,)),
        ],
        compiler_params=pltpu.CompilerParams(vmem_limit_bytes=60 << 20),
        name="weight_pack",
    )(weights)


def minmod(a, b):
    return jnp.maximum(jnp.minimum(a, b), 0.0) + jnp.minimum(jnp.maximum(a, b), 0.0)


def cons_of(p):
    rho, u, v, w, pr = p
    ke = u * u + v * v + w * w
    return [rho, rho * u, rho * v, rho * w, pr * (1.0 / (GAS_GAMMA - 1.0)) + 0.5 * rho * ke]


def face_parts(p, n):
    cons = cons_of(p)
    un, pr = p[1 + n], p[4]
    flux = [c * un for c in cons]
    flux[1 + n] = flux[1 + n] + pr
    flux[4] = flux[4] + pr * un
    gp = GAS_GAMMA * pr
    speed = jnp.abs(un) + gp * lax.rsqrt(gp * p[0])
    return cons, flux, speed


def rusanov2(low, up, n):
    c0, f0, s0 = face_parts(low, n)
    c1, f1, s1 = face_parts(up, n)
    wave = jnp.maximum(s0, s1)
    return [(f0[i] + f1[i]) - wave * (c1[i] - c0[i]) for i in range(5)]


def rolled_divergence(p, axis, n, keep=None):
    length = p[0].shape[axis]

    def back(v):
        return pltpu.roll(v, 1, axis)

    def ahead(v):
        return pltpu.roll(v, length - 1, axis)

    low, up = [], []
    for v in p:
        d = v - back(v)
        half = 0.5 * minmod(d, ahead(d))
        low.append(v + half)
        up.append(ahead(v - half))
    flux = rusanov2(low, up, n)
    if keep is not None:
        flux = [jnp.where(keep, f, 0.0) for f in flux]
    return [f - back(f) for f in flux]


def cell_parts(c):
    row = (c >> 11) * 8 + ((c >> 7) & 7)
    lane = ((c >> 10) & 1) * 128 + (c & 127)
    return row, lane


def one_hot(ids, size):
    width = ids.shape[1]
    return lax.broadcasted_iota(jnp.int32, (size, width), 0) == ids


def two_parts(v):
    hi = v.astype(BF16)
    return hi, (v - hi.astype(F32)).astype(BF16)


def flux_kernel(
    dp_ref, vel_ref, cut_ref, xlo_ref, xhi_ref, cell_ref, base_ref, val_ref, edge_ref, scale_ref,
    xe, dl,
):
    for comp in range(5):
        ref, k = comp_ref(dp_ref, vel_ref, comp)
        xe[comp, 0:32] = xlo_ref[comp]
        xe[comp, 32:160] = ref[k]
        xe[comp, 160:192] = xhi_ref[comp]
        for j, row in enumerate((0, 1, 2, 13, 14, 15)):
            edge_ref[comp, j] = ref[k, pl.ds(row, 8, stride=16), :]
    for j, row in enumerate((0, 1, 14, 15)):
        cut = cut_ref[pl.ds(row, 8, stride=16), :].astype(F32)
        scale_ref[j] = (-2.0 * STEP_RATIO) / (1.0 + cut)

    def plane(j):
        return [xe[c, pl.ds(pl.multiple_of(j * 16, 16), 16), :] for c in range(5)]

    def face_x(j):
        a, b, c, d = plane(j - 1), plane(j), plane(j + 1), plane(j + 2)
        low, up = [], []
        for i in range(5):
            mid = c[i] - b[i]
            low.append(b[i] + 0.5 * minmod(b[i] - a[i], mid))
            up.append(c[i] - 0.5 * minmod(mid, d[i] - c[i]))
        return rusanov2(low, up, 0)

    row_id = lax.broadcasted_iota(jnp.int32, (16, 128), 0)
    inner = (row_id >= 1) & (row_id <= 13)

    def body(x, before):
        after = face_x(x + 2)
        centre = plane(x + 2)
        ydiv = rolled_divergence(centre, 0, 1, inner)
        zdiv = rolled_divergence(centre, 1, 2)
        here = pl.ds(pl.multiple_of(x * 16, 16), 16)
        scale = (-2.0 * STEP_RATIO) / (1.0 + cut_ref[here, :].astype(F32))
        cons = cons_of(centre)
        for i in range(5):
            delta = scale * ((after[i] - before[i]) + zdiv[i] + ydiv[i])
            base_ref[i, here, :] = cons[i] + delta
            row = pl.multiple_of(i * 64 + x * 8, 8)
            dl[pl.ds(row, 8), 0:128] = delta[0:8]
            dl[pl.ds(row, 8), 128:256] = delta[8:16]
        return after

    lax.fori_loop(0, 8, body, face_x(1))

    whole = dl[...]
    hi = whole.astype(BF16)
    rest = whole - hi.astype(F32)
    mid, low = two_parts(rest)
    pieces = jnp.concatenate([hi, mid, low], axis=0)
    for q in range(8):
        row, lane = cell_parts(cell_ref[q : q + 1, :])
        lane_hot = one_hot(lane, 256).astype(F32).astype(BF16)
        got = jnp.dot(pieces, lane_hot, preferred_element_type=F32)
        got = got[0:320] + (got[320:640] + got[640:960])
        row_hot = one_hot(row, 64)
        rows = [
            jnp.sum(jnp.where(row_hot, got[v * 64 : v * 64 + 64], 0.0), axis=0, keepdims=True)
            for v in range(5)
        ]
        val_ref[q] = jnp.concatenate(rows + [jnp.zeros((3, 256), F32)], axis=0)


def fluxes(dens_pres, velocity, cut_class, xlo, xhi, cells):
    return pl.pallas_call(
        flux_kernel,
        out_shape=(
            jax.ShapeDtypeStruct((5, 128, 128), F32),
            jax.ShapeDtypeStruct((8, 8, 256), F32),
            jax.ShapeDtypeStruct((5, 6, 8, 128), F32),
            jax.ShapeDtypeStruct((4, 8, 128), F32),
        ),
        in_specs=[VMEM_SPEC] * 6,
        out_specs=(VMEM_SPEC,) * 4,
        scratch_shapes=[pltpu.VMEM((5, 192, 128), F32), pltpu.VMEM((320, 256), F32)],
        compiler_params=PARAMS,
        name="flux_gather",
    )(dens_pres, velocity, cut_class, xlo, xhi, cells)


def edge_kernel(
    rank_ref, edge_ref, scale_ref, ylo_ref, yhi_ref, cell_ref, part_ref, fix_ref, val_ref, lhs_ref
):
    def halo(ref, j):
        return [ref[c * 16 + j * 8 : c * 16 + j * 8 + 8, :] for c in range(5)]

    def own(j):
        return [edge_ref[c, j] for c in range(5)]

    def two_faces(rows):
        low, up = [], []
        for k in (1, 2, 3):
            half = [
                0.5 * minmod(rows[k][c] - rows[k - 1][c], rows[k + 1][c] - rows[k][c])
                for c in range(5)
            ]
            low.append([rows[k][c] + half[c] for c in range(5)])
            up.append([rows[k][c] - half[c] for c in range(5)])
        return rusanov2(low[0], up[1], 1), rusanov2(low[1], up[2], 1)

    face_a, face_b = two_faces([halo(ylo_ref, 0), halo(ylo_ref, 1), own(0), own(1), own(2)])
    face_c, face_d = two_faces([own(3), own(4), own(5), halo(yhi_ref, 0), halo(yhi_ref, 1)])
    fix = []
    for c in range(5):
        fix.append(
            [
                scale_ref[0] * (face_b[c] - face_a[c]),
                -scale_ref[1] * face_b[c],
                scale_ref[2] * face_c[c],
                scale_ref[3] * (face_d[c] - face_c[c]),
            ]
        )
        for j in range(4):
            fix_ref[c, j] = fix[c][j]
    table = jnp.concatenate(
        [
            jnp.concatenate([fix[c][j], fix[c][j + 2]], axis=1)
            for c in range(5)
            for j in range(2)
        ],
        axis=0,
    )
    pieces = jnp.concatenate(two_parts(table), axis=0)
    half_id = lax.broadcasted_iota(jnp.int32, (8, 128), 1) // 64
    for q in range(8):
        cell = cell_ref[q : q + 1, :]
        x, y, z = cell >> 11, (cell >> 7) & 15, cell & 127
        on_edge = (y < 2) | (y > 13)
        row = jnp.where(on_edge, (y & 1) * 8 + x, -1)
        lane = (y >> 3) * 128 + z
        got = jnp.dot(pieces, one_hot(lane, 256).astype(F32).astype(BF16), preferred_element_type=F32)
        got = got[0:80] + got[80:160]
        row_hot = one_hot(row, 16)
        rows = [
            jnp.sum(jnp.where(row_hot, got[c * 16 : c * 16 + 16], 0.0), axis=0, keepdims=True)
            for c in range(5)
        ]
        val = part_ref[q] + jnp.concatenate(rows + [jnp.zeros((3, 256), F32)], axis=0)
        val_ref[q] = val
        placed = []
        for t in range(4):
            piece = val[:, (t // 2) * 128 : (t // 2) * 128 + 128]
            rank = rank_ref[q * 4 + t]
            moved = jnp.where(rank == t % 2, piece, pltpu.roll(piece, 64, 1))
            placed.append(jnp.where(half_id == rank, moved, 0.0))
        both = jnp.concatenate(two_parts(jnp.concatenate(placed, axis=0)), axis=0)
        lhs_ref[q] = jnp.concatenate([both, both], axis=1)


def edges(ranks, edge, scale, ylo, yhi, cells, part):
    return pl.pallas_call(
        edge_kernel,
        out_shape=(
            jax.ShapeDtypeStruct((5, 4, 8, 128), F32),
            jax.ShapeDtypeStruct((8, 8, 256), F32),
            jax.ShapeDtypeStruct((8, 64, 256), BF16),
        ),
        in_specs=[SMEM_SPEC] + [VMEM_SPEC] * 6,
        out_specs=(VMEM_SPEC,) * 3,
        compiler_params=PARAMS,
        name="edge_gather",
    )(ranks, edge, scale, ylo, yhi, cells, part)


def contract_last(a, b):
    return lax.dot_general(a, b, (((1,), (1,)), ((), ())), preferred_element_type=F32)


def mix_kernel(
    helper_ref, live_ref, w_ref, lhs_ref, val_ref, cell_ref, base_ref, fix_ref, out_ref
):
    live = live_ref[0]
    slot_of = lax.broadcasted_iota(jnp.int32, (8, 256), 1) // 64
    total = jnp.zeros((320, 256), F32)
    for q in range(8):
        tiles = []
        for t in range(4):
            w_hi, w_lo = two_parts(w_ref[helper_ref[q * 4 + t]])
            tiles.append(jnp.concatenate([w_hi, w_lo], axis=1))
        made = contract_last(lhs_ref[q], jnp.concatenate(tiles, axis=0))
        made = made[0:32] + made[32:64]
        mixed = made[0:8]
        for t in range(1, 4):
            mixed = jnp.where(slot_of == t, made[t * 8 : t * 8 + 8], mixed)
        diff = jnp.where(q * 4 + slot_of < live, mixed - val_ref[q], 0.0)
        d_hi = diff.astype(BF16).astype(F32)
        d_lo = diff - d_hi
        row, lane = cell_parts(cell_ref[q : q + 1, :])
        row_hot = one_hot(row, 64)
        lane_hot = one_hot(lane, 256).astype(F32).astype(BF16)
        spread = [
            jnp.concatenate(
                [jnp.where(row_hot, d[v : v + 1, :], 0.0).astype(BF16) for v in range(5)], axis=0
            )
            for d in (d_hi, d_lo)
        ]
        total = total + contract_last(spread[0], lane_hot) + contract_last(spread[1], lane_hot)
    for v in range(5):
        for x in range(8):
            row = v * 64 + x * 8
            top = slice(x * 16, x * 16 + 8)
            bottom = slice(x * 16 + 8, x * 16 + 16)
            out_ref[v, top, :] = base_ref[v, top, :] + total[row : row + 8, 0:128]
            out_ref[v, bottom, :] = base_ref[v, bottom, :] + total[row : row + 8, 128:256]
        for j, y in enumerate((0, 1, 14, 15)):
            rows = pl.ds(y, 8, stride=16)
            out_ref[v, rows, :] = out_ref[v, rows, :] + fix_ref[v, j]


def redistribute(helpers, live, weights, lhs, val, cells, base, fix):
    return pl.pallas_call(
        mix_kernel,
        out_shape=jax.ShapeDtypeStruct(base.shape, F32),
        in_specs=[SMEM_SPEC] * 2 + [VMEM_SPEC] * 6,
        out_specs=VMEM_SPEC,
        compiler_params=PARAMS,
        name="mix_scatter",
    )(helpers, live, weights, lhs, val, cells, base, fix)


def local(dens_pres, velocity, cut_class, nbhd_cells, helper_list, live_counts, redist_weights):
    ngx, ngy = lax.axis_size("gx"), lax.axis_size("gy")
    dens_pres = dens_pres.reshape(2, 128, 128)
    velocity = velocity.reshape(3, 128, 128)
    cut_class = cut_class.reshape(128, 128)
    packed = pack_weights(redist_weights[0, 0])
    weights = lax.all_to_all(packed, "gy", split_axis=0, concat_axis=0, tiled=True)
    xhead, xtail, yhead, ytail = pack_halo(dens_pres, velocity)
    up_x = [(i, (i + 1) % ngx) for i in range(ngx)]
    up_y = [(i, (i + 1) % ngy) for i in range(ngy)]
    ylo = lax.ppermute(ytail, "gy", up_y)
    yhi = lax.ppermute(yhead, "gy", [(b, a) for a, b in up_y])
    xlo = lax.ppermute(xtail, "gx", up_x)
    xhi = lax.ppermute(xhead, "gx", [(b, a) for a, b in up_x])
    helpers = helper_list[0, 0]
    slots = helpers.shape[0]
    same = helpers[None, :] == helpers[:, None]
    below = lax.broadcasted_iota(jnp.int32, (slots, slots), 1) < lax.broadcasted_iota(
        jnp.int32, (slots, slots), 0
    )
    ranks = jnp.sum((same & below).astype(jnp.int32), axis=1)
    cells = nbhd_cells.reshape(8, 256)
    base, part, edge, scale = fluxes(dens_pres, velocity, cut_class, xlo, xhi, cells)
    fix, val, lhs = edges(ranks, edge, scale, ylo, yhi, cells, part)
    out = redistribute(helpers, live_counts[0], weights, lhs, val, cells, base, fix)
    return out.reshape(5, 8, 16, 128)


def solution(mesh):
    in_specs = (
        P(None, "gx", "gy", None),
        P(None, "gx", "gy", None),
        P("gx", "gy", None),
        P("gx", "gy", None, None),
        P("gx", "gy", None),
        P("gx", "gy"),
        P("gx", "gy", None, None, None, None),
    )
    out_specs = P(None, "gx", "gy", None)
    return jax.shard_map(local, mesh=mesh, in_specs=in_specs, out_specs=out_specs, check_vma=False)
```

time: 58.1 us -> 48.9 us (0.84)
  the two profiles are of different devices: /device:TPU:48 before, /device:TPU:16 now
where the time goes in v2:
time: 48.9 us; the launch traced here: 48.7 us
  starting transfers between devices  24.1 us (49%)
  waiting for transfers between devices  12.6 us (26%)
  Pallas kernels  11 us (22%)
  between operations  0.78 us (2%)
    all_to_all x1, starting transfers between devices, local(): lax.all_to_all(packed, 'gy', split_axis=0, concat_axis=0, tiled=True)  13.2 us
    ppermute x1, waiting for transfers between devices, local(): ylo = lax.ppermute(ytail, 'gy', up_y)  12.6 us
    ppermute x1, starting transfers between devices, local(): yhi = lax.ppermute(yhead, 'gy', [(b, a) for a, b in up_y])  5.46 us
    pallas_call x1, Pallas kernels, fluxes(): pl.pallas_call(flux_kernel, out_shape=(jax.ShapeDtypeStruct((5, 128, 128)...  3.92 us
    ppermute x1, starting transfers between devices, local(): ylo = lax.ppermute(ytail, 'gy', up_y)  3.69 us
    pallas_call x1, Pallas kernels, redistribute(): pl.pallas_call(mix_kernel, out_shape=jax.ShapeDtypeStruct(base.shape, F32...  3.33 us
    pallas_call x1, Pallas kernels, pack_weights(): pl.pallas_call(weight_kernel, out_shape=jax.ShapeDtypeStruct((blocks, n,...  2.6 us
    ppermute x1, starting transfers between devices, local(): xhi = lax.ppermute(xhead, 'gx', [(b, a) for a, b in up_x])  1.73 us
  transfers between devices with their start and end apart: 5, of which 1 were waited for; matrix products, arithmetic and copies ran while one was open for 1% of the time, Pallas kernels for 10%

profile of v2, /device:TPU:16, one launch (start us, length us, event | category | flops | bytes accessed | tf_op | source)
XLA Modules:
  0.0 48.7 jit_solution(8916528565264020769)
XLA Ops:
  0.0 0.0 copy-start
  0.0 0.0 copy-start.1
  0.0 0.0 copy-start.3
  0.0 0.0 copy-start.4
  0.0 0.0 copy-start.2
  0.0 2.6 %weight_pack.1 = f32[32,64,128]{2,1,0:T(8,128)} custom-call(f32[32,2,64,64]{3,2,1,0:T(8,128)} %bitcast.17), custom_call_target="tpu_custom_call" | custom-call | tf_op jit(solution)/shard_map/weight_pack/pallas_call | solution.py:71
  2.6 13.2 %all-to-all-start = ((f32[32,64,128]{2,1,0:T(8,128)}), f32[32,64,128]{2,1,0:T(8,128)S(1)}, u32[]{:S(2)}, u32[]{:S(2)}) async-start(f32[32,64,128]{2,1,0:T(8,128)} %weight_pack.1), calls=%async_computation | async-start | bytes 2097152 | tf_op jit(solution)/shard_map/all_to_all | solution.py:381
  15.8 0.0 copy-done
  15.8 0.0 copy-done.1
  15.9 0.0 collective-permute-start
  15.9 1.7 %collective-permute-start.1 = (f32[5,32,128]{2,1,0:T(8,128)S(1)}, f32[5,32,128]{2,1,0:T(8,128)S(1)}, u32[]{:S(2)}, u32[]{:S(2)}) collective-permute-start(f32[5,32,128]{2,1,0:T(8,128)S(1)} %get-tuple-element.17), channel_id=1, source_target_pairs={{32,0},{64,32},{96,64},{128,96},{160,128},{192,160},{224,192},{256... | collective-permute-start | bytes 245768 | tf_op jit(solution)/shard_map/ppermute | solution.py:388
  17.6 3.7 %collective-permute-start.2 = (f32[80,128]{1,0:T(8,128)S(1)}, f32[80,128]{1,0:T(8,128)S(1)}, u32[]{:S(2)}, u32[]{:S(2)}) collective-permute-start(f32[80,128]{1,0:T(8,128)S(1)} %get-tuple-element.20), channel_id=1, source_target_pairs={{0,1},{1,2},{2,3},{3,4},{4,5},{5,6},{6,7},{7,8},{8,9},{9,10},{10,1... | collective-permute-start | bytes 122888 | tf_op jit(solution)/shard_map/ppermute | solution.py:385
  21.3 5.5 %collective-permute-start.3 = (f32[80,128]{1,0:T(8,128)S(1)}, f32[80,128]{1,0:T(8,128)S(1)}, u32[]{:S(2)}, u32[]{:S(2)}) collective-permute-start(f32[80,128]{1,0:T(8,128)S(1)} %get-tuple-element.21), channel_id=1, source_target_pairs={{1,0},{2,1},{3,2},{4,3},{5,4},{6,5},{7,6},{8,7},{9,8},{10,9},{11,1... | collective-permute-start | bytes 122888 | tf_op jit(solution)/shard_map/ppermute | solution.py:386
  26.8 0.0 copy-done.3
  26.8 0.2 convert_reduce_fusion.rank_ref
  27.7 0.0 copy-done.4
  27.7 0.1 reshape.20.cell_ref
  27.7 0.0 collective-permute-done.xlo_ref
  27.7 0.0 collective-permute-done.1.xhi_ref
  27.7 0.0 copy-done.2
  27.8 3.9 %flux_gather.1 = (f32[5,128,128]{2,1,0:T(8,128)S(1)}, f32[8,8,256]{2,1,0:T(8,128)S(1)}, f32[5,6,8,128]{3,2,1,0:T(8,128)S(1)}, f32[4,8,128]{2,1,0:T(8,128)S(1)}) custom-call(f32[2,128,128]{2,1,0:T(8,128)S(1)} %bitcast.13, f32[3,128,128]{2,1,0:T(8,128)S(1)} %bitcast.11, s32[128,128]{1,0:T(8,128)S(1)} %bitcast.14, ...), custom_call_target="tpu_custom_call" | custom-call | tf_op jit(solution)/shard_map/flux_gather/pallas_call | solution.py:219
  31.7 12.6 %collective-permute-done.2.ylo_ref = f32[80,128]{1,0:T(8,128)S(1)} collective-permute-done((f32[80,128]{1,0:T(8,128)S(1)}, f32[80,128]{1,0:T(8,128)S(1)}, u32[]{:S(2)}, u32[]{:S(2)}) %collective-permute-start.2) | collective-permute-done | bytes 40992 | tf_op jit(solution)/shard_map/ppermute | solution.py:385
  44.2 0.0 collective-permute-done.3.yhi_ref
  44.2 1.1 %edge_gather.1 = (f32[5,4,8,128]{3,2,1,0:T(8,128)S(1)}, f32[8,8,256]{2,1,0:T(8,128)S(1)}, bf16[8,64,256]{2,1,0:T(8,128)(2,1)S(1)}) custom-call(s32[32]{0:T(128)S(1)} %convert_reduce_fusion.rank_ref, f32[5,6,8,128]{3,2,1,0:T(8,128)S(1)} %get-tuple-element.18.edge_ref, f32[4,8,128]{2,1,0:T(8,128)S(1)} %get-tuple-element.19.scale_ref, ...), custom_call_target="tpu_custom_call" | custom-call | tf_op jit(solution)/shard_map/edge_gather/pallas_call | solution.py:305
  45.3 0.0 all-to-all-done.w_ref
  45.3 3.3 %mix_scatter.1 = f32[5,128,128]{2,1,0:T(8,128)} custom-call(s32[32]{0:T(128)S(1)} %bitcast.16, s32[1]{0:T(128)} %bitcast.9.live_ref, f32[32,64,128]{2,1,0:T(8,128)S(1)} %all-to-all-done.w_ref, bf16[8,64,256]{2,1,0:T(8,128)(2,1)S(1)} %get-tuple-element.23.lhs_ref, f32[8,8,256]{2,1,0:T(8,128)S(1)} %get-tuple-element.24.val_ref, ...), custom_call_target="tpu_custom_call" | custom-call | tf_op jit(solution)/shard_map/mix_scatter/pallas_call | solution.py:365
  (1 shorter events, 0.0 us)
Async XLA Ops:
  0.0 15.8 %copy-start = (f32[3,8,16,128]{3,2,1,0:T(8,128)S(1)}, f32[3,8,16,128]{3,2,1,0:T(8,128)}, u32[]{:S(2)}) copy-start(f32[3,8,16,128]{3,2,1,0:T(8,128)} %param.8) | copy-start | bytes 589828
  0.0 15.8 %copy-start.1 = (f32[2,8,16,128]{3,2,1,0:T(8,128)S(1)}, f32[2,8,16,128]{3,2,1,0:T(8,128)}, u32[]{:S(2)}) copy-start(f32[2,8,16,128]{3,2,1,0:T(8,128)} %param.7) | copy-start | bytes 393220
  0.0 26.8 %copy-start.3 = (s32[1,1,32]{2,1,0:T(1,128)S(1)}, s32[1,1,32]{2,1,0:T(1,128)}, u32[]{:S(2)}) copy-start(s32[1,1,32]{2,1,0:T(1,128)} %param.11) | copy-start | bytes 388
  0.0 27.7 %copy-start.4 = (s32[1,1,32,64]{3,2,1,0:T(8,128)S(1)}, s32[1,1,32,64]{3,2,1,0:T(8,128)}, u32[]{:S(2)}) copy-start(s32[1,1,32,64]{3,2,1,0:T(8,128)} %param.10) | copy-start | bytes 24580
  0.0 27.7 %copy-start.2 = (s32[8,16,128]{2,1,0:T(8,128)S(1)}, s32[8,16,128]{2,1,0:T(8,128)}, u32[]{:S(2)}) copy-start(s32[8,16,128]{2,1,0:T(8,128)} %param.9) | copy-start | bytes 196612
  2.6 42.7 %all-to-all-start = ((f32[32,64,128]{2,1,0:T(8,128)}), f32[32,64,128]{2,1,0:T(8,128)S(1)}, u32[]{:S(2)}, u32[]{:S(2)}) async-start(f32[32,64,128]{2,1,0:T(8,128)} %weight_pack.1), calls=%async_computation | async-start | bytes 2097152 | tf_op jit(solution)/shard_map/all_to_all | solution.py:381
  15.9 11.9 %collective-permute-start = (f32[5,32,128]{2,1,0:T(8,128)S(1)}, f32[5,32,128]{2,1,0:T(8,128)S(1)}, u32[]{:S(2)}, u32[]{:S(2)}) collective-permute-start(f32[5,32,128]{2,1,0:T(8,128)S(1)} %get-tuple-element.16), channel_id=1, source_target_pairs={{0,32},{32,64},{64,96},{96,128},{128,160},{160,192},{192,224},{224... | collective-permute-start | bytes 245768 | tf_op jit(solution)/shard_map/ppermute | solution.py:387
  15.9 11.8 %collective-permute-start.1 = (f32[5,32,128]{2,1,0:T(8,128)S(1)}, f32[5,32,128]{2,1,0:T(8,128)S(1)}, u32[]{:S(2)}, u32[]{:S(2)}) collective-permute-start(f32[5,32,128]{2,1,0:T(8,128)S(1)} %get-tuple-element.17), channel_id=1, source_target_pairs={{32,0},{64,32},{96,64},{128,96},{160,128},{192,160},{224,192},{256... | collective-permute-start | bytes 245768 | tf_op jit(solution)/shard_map/ppermute | solution.py:388
  17.6 26.6 %collective-permute-start.2 = (f32[80,128]{1,0:T(8,128)S(1)}, f32[80,128]{1,0:T(8,128)S(1)}, u32[]{:S(2)}, u32[]{:S(2)}) collective-permute-start(f32[80,128]{1,0:T(8,128)S(1)} %get-tuple-element.20), channel_id=1, source_target_pairs={{0,1},{1,2},{2,3},{3,4},{4,5},{5,6},{6,7},{7,8},{8,9},{9,10},{10,1... | collective-permute-start | bytes 122888 | tf_op jit(solution)/shard_map/ppermute | solution.py:385
  21.3 22.9 %collective-permute-start.3 = (f32[80,128]{1,0:T(8,128)S(1)}, f32[80,128]{1,0:T(8,128)S(1)}, u32[]{:S(2)}, u32[]{:S(2)}) collective-permute-start(f32[80,128]{1,0:T(8,128)S(1)} %get-tuple-element.21), channel_id=1, source_target_pairs={{1,0},{2,1},{3,2},{4,3},{5,4},{6,5},{7,6},{8,7},{9,8},{10,9},{11,1... | collective-permute-start | bytes 122888 | tf_op jit(solution)/shard_map/ppermute | solution.py:386

commit v3 on v2

--- a/solution.py
+++ b/solution.py
@@ -76,8 +76,8 @@
         scratch_shapes=[
             pltpu.VMEM(weights.shape, F32),
             pltpu.VMEM((blocks, n, cap * n), F32),
-            pltpu.SemaphoreType.DMA((8,)),
-            pltpu.SemaphoreType.DMA((8,)),
+            pltpu.SemaphoreType.DMA((4,)),
+            pltpu.SemaphoreType.DMA((4,)),
         ],
         compiler_params=pltpu.CompilerParams(vmem_limit_bytes=60 << 20),
         name="weight_pack",
@@ -150,9 +150,14 @@
 
 
 def flux_kernel(
-    dp_ref, vel_ref, cut_ref, xlo_ref, xhi_ref, cell_ref, base_ref, val_ref, edge_ref, scale_ref,
-    xe, dl,
+    rank_ref, live_ref, dp_ref, vel_ref, cut_ref, xlo_ref, xhi_ref, cell_ref,
+    base_ref, val_ref, edge_ref, scale_ref, half_ref, live_out_ref, xe, dl,
 ):
+    for s in range(32):
+        half_ref[s : s + 1, :] = jnp.full((1, 128), rank_ref[s], jnp.int32)
+    slot = lax.broadcasted_iota(jnp.int32, (8, 256), 0) * 4
+    slot = slot + lax.broadcasted_iota(jnp.int32, (8, 256), 1) // 64
+    live_out_ref[...] = jnp.where(slot < live_ref[0], 1.0, 0.0)
     for comp in range(5):
         ref, k = comp_ref(dp_ref, vel_ref, comp)
         xe[comp, 0:32] = xlo_ref[comp]
@@ -215,7 +220,7 @@
         val_ref[q] = jnp.concatenate(rows + [jnp.zeros((3, 256), F32)], axis=0)
 
 
-def fluxes(dens_pres, velocity, cut_class, xlo, xhi, cells):
+def fluxes(ranks, live, dens_pres, velocity, cut_class, xlo, xhi, cells):
     return pl.pallas_call(
         flux_kernel,
         out_shape=(
@@ -223,17 +228,20 @@
             jax.ShapeDtypeStruct((8, 8, 256), F32),
             jax.ShapeDtypeStruct((5, 6, 8, 128), F32),
             jax.ShapeDtypeStruct((4, 8, 128), F32),
+            jax.ShapeDtypeStruct((32, 128), jnp.int32),
+            jax.ShapeDtypeStruct((8, 256), F32),
         ),
-        in_specs=[VMEM_SPEC] * 6,
-        out_specs=(VMEM_SPEC,) * 4,
+        in_specs=[SMEM_SPEC] * 2 + [VMEM_SPEC] * 6,
+        out_specs=(VMEM_SPEC,) * 6,
         scratch_shapes=[pltpu.VMEM((5, 192, 128), F32), pltpu.VMEM((320, 256), F32)],
         compiler_params=PARAMS,
         name="flux_gather",
-    )(dens_pres, velocity, cut_class, xlo, xhi, cells)
+    )(ranks, live, dens_pres, velocity, cut_class, xlo, xhi, cells)
 
 
 def edge_kernel(
-    rank_ref, edge_ref, scale_ref, ylo_ref, yhi_ref, cell_ref, part_ref, fix_ref, val_ref, lhs_ref
+    half_ref, live_ref, edge_ref, scale_ref, ylo_ref, yhi_ref, cell_ref, part_ref,
+    fix_ref, val_ref, lhs_ref,
 ):
     def halo(ref, j):
         return [ref[c * 16 + j * 8 : c * 16 + j * 8 + 8, :] for c in range(5)]
@@ -290,18 +298,19 @@
             for c in range(5)
         ]
         val = part_ref[q] + jnp.concatenate(rows + [jnp.zeros((3, 256), F32)], axis=0)
+        val = jnp.where(live_ref[q : q + 1, :] > 0.0, val, 0.0)
         val_ref[q] = val
         placed = []
         for t in range(4):
             piece = val[:, (t // 2) * 128 : (t // 2) * 128 + 128]
-            rank = rank_ref[q * 4 + t]
+            rank = half_ref[q * 4 + t : q * 4 + t + 1, :]
             moved = jnp.where(rank == t % 2, piece, pltpu.roll(piece, 64, 1))
             placed.append(jnp.where(half_id == rank, moved, 0.0))
         both = jnp.concatenate(two_parts(jnp.concatenate(placed, axis=0)), axis=0)
         lhs_ref[q] = jnp.concatenate([both, both], axis=1)
 
 
-def edges(ranks, edge, scale, ylo, yhi, cells, part):
+def edges(half, live, edge, scale, ylo, yhi, cells, part):
     return pl.pallas_call(
         edge_kernel,
         out_shape=(
@@ -309,11 +318,11 @@
             jax.ShapeDtypeStruct((8, 8, 256), F32),
             jax.ShapeDtypeStruct((8, 64, 256), BF16),
         ),
-        in_specs=[SMEM_SPEC] + [VMEM_SPEC] * 6,
+        in_specs=[VMEM_SPEC] * 8,
         out_specs=(VMEM_SPEC,) * 3,
         compiler_params=PARAMS,
         name="edge_gather",
-    )(ranks, edge, scale, ylo, yhi, cells, part)
+    )(half, live, edge, scale, ylo, yhi, cells, part)
 
 
 def contract_last(a, b):
@@ -321,55 +330,75 @@
 
 
 def mix_kernel(
-    helper_ref, live_ref, w_ref, lhs_ref, val_ref, cell_ref, base_ref, fix_ref, out_ref
+    helper_ref, w_ref, lhs_ref, val_ref, cell_ref, base_ref, fix_ref, out_ref,
+    helper, made, helper_sem, out_sems,
 ):
-    live = live_ref[0]
+    fetch = pltpu.make_async_copy(helper_ref, helper, helper_sem)
+    fetch.start()
     slot_of = lax.broadcasted_iota(jnp.int32, (8, 256), 1) // 64
-    total = jnp.zeros((320, 256), F32)
+    lane_hots, row_hots = [], []
+    for q in range(8):
+        row, lane = cell_parts(cell_ref[q : q + 1, :])
+        row_hots.append(one_hot(row, 64))
+        lane_hots.append(one_hot(lane, 256).astype(F32).astype(BF16))
+    fetch.wait()
+    diffs = []
     for q in range(8):
         tiles = []
         for t in range(4):
-            w_hi, w_lo = two_parts(w_ref[helper_ref[q * 4 + t]])
+            w_hi, w_lo = two_parts(w_ref[helper[q * 4 + t]])
             tiles.append(jnp.concatenate([w_hi, w_lo], axis=1))
-        made = contract_last(lhs_ref[q], jnp.concatenate(tiles, axis=0))
-        made = made[0:32] + made[32:64]
-        mixed = made[0:8]
+        got = contract_last(lhs_ref[q], jnp.concatenate(tiles, axis=0))
+        got = got[0:32] + got[32:64]
+        mixed = got[0:8]
         for t in range(1, 4):
-            mixed = jnp.where(slot_of == t, made[t * 8 : t * 8 + 8], mixed)
-        diff = jnp.where(q * 4 + slot_of < live, mixed - val_ref[q], 0.0)
-        d_hi = diff.astype(BF16).astype(F32)
-        d_lo = diff - d_hi
-        row, lane = cell_parts(cell_ref[q : q + 1, :])
-        row_hot = one_hot(row, 64)
-        lane_hot = one_hot(lane, 256).astype(F32).astype(BF16)
+            mixed = jnp.where(slot_of == t, got[t * 8 : t * 8 + 8], mixed)
+        diffs.append(mixed - val_ref[q])
+    columns = []
+    for q in range(8):
+        d_hi = diffs[q].astype(BF16).astype(F32)
         spread = [
-            jnp.concatenate(
-                [jnp.where(row_hot, d[v : v + 1, :], 0.0).astype(BF16) for v in range(5)], axis=0
-            )
-            for d in (d_hi, d_lo)
+            jnp.where(row_hots[q], d[v : v + 1, :], 0.0).astype(BF16)
+            for d in (d_hi, diffs[q] - d_hi)
+            for v in range(5)
         ]
-        total = total + contract_last(spread[0], lane_hot) + contract_last(spread[1], lane_hot)
+        columns.append(jnp.concatenate(spread, axis=0))
+    both = contract_last(jnp.concatenate(columns, axis=1), jnp.concatenate(lane_hots, axis=1))
+    total = both[0:320] + both[320:640]
+
+    def store(v):
+        return pltpu.make_async_copy(made.at[v], out_ref.at[v], out_sems.at[v])
+
     for v in range(5):
         for x in range(8):
             row = v * 64 + x * 8
             top = slice(x * 16, x * 16 + 8)
             bottom = slice(x * 16 + 8, x * 16 + 16)
-            out_ref[v, top, :] = base_ref[v, top, :] + total[row : row + 8, 0:128]
-            out_ref[v, bottom, :] = base_ref[v, bottom, :] + total[row : row + 8, 128:256]
+            made[v, top, :] = base_ref[v, top, :] + total[row : row + 8, 0:128]
+            made[v, bottom, :] = base_ref[v, bottom, :] + total[row : row + 8, 128:256]
         for j, y in enumerate((0, 1, 14, 15)):
             rows = pl.ds(y, 8, stride=16)
-            out_ref[v, rows, :] = out_ref[v, rows, :] + fix_ref[v, j]
-
-
-def redistribute(helpers, live, weights, lhs, val, cells, base, fix):
+            made[v, rows, :] = made[v, rows, :] + fix_ref[v, j]
+        store(v).start()
+    for v in range(5):
+        store(v).wait()
+
+
+def redistribute(helpers, weights, lhs, val, cells, base, fix):
     return pl.pallas_call(
         mix_kernel,
         out_shape=jax.ShapeDtypeStruct(base.shape, F32),
-        in_specs=[SMEM_SPEC] * 2 + [VMEM_SPEC] * 6,
-        out_specs=VMEM_SPEC,
+        in_specs=[ANY_SPEC] + [VMEM_SPEC] * 6,
+        out_specs=ANY_SPEC,
+        scratch_shapes=[
+            pltpu.SMEM((32,), jnp.int32),
+            pltpu.VMEM((5, 128, 128), F32),
+            pltpu.SemaphoreType.DMA,
+            pltpu.SemaphoreType.DMA((5,)),
+        ],
         compiler_params=PARAMS,
         name="mix_scatter",
-    )(helpers, live, weights, lhs, val, cells, base, fix)
+    )(helpers, weights, lhs, val, cells, base, fix)
 
 
 def local(dens_pres, velocity, cut_class, nbhd_cells, helper_list, live_counts, redist_weights):
@@ -394,9 +423,11 @@
     )
     ranks = jnp.sum((same & below).astype(jnp.int32), axis=1)
     cells = nbhd_cells.reshape(8, 256)
-    base, part, edge, scale = fluxes(dens_pres, velocity, cut_class, xlo, xhi, cells)
-    fix, val, lhs = edges(ranks, edge, scale, ylo, yhi, cells, part)
-    out = redistribute(helpers, live_counts[0], weights, lhs, val, cells, base, fix)
+    base, part, edge, scale, half, live = fluxes(
+        ranks, live_counts[0], dens_pres, velocity, cut_class, xlo, xhi, cells
+    )
+    fix, val, lhs = edges(half, live, edge, scale, ylo, yhi, cells, part)
+    out = redistribute(helpers, weights, lhs, val, cells, base, fix)
     return out.reshape(5, 8, 16, 128)
 
 

time: 48.9 us -> 47.8 us (0.978)
  the two profiles are of different devices: /device:TPU:16 before, /device:TPU:32 now
where the time goes in v3:
time: 47.8 us; the launch traced here: 47.5 us
  starting transfers between devices  25.3 us (53%)
  waiting for transfers between devices  11.2 us (23%)
  Pallas kernels  9.96 us (21%)
  between operations  0.78 us (2%)
    all_to_all x1, starting transfers between devices, local(): lax.all_to_all(packed, 'gy', split_axis=0, concat_axis=0, tiled=True)  13.2 us
    ppermute x1, waiting for transfers between devices, local(): ylo = lax.ppermute(ytail, 'gy', up_y)  10.8 us
    ppermute x1, starting transfers between devices, local(): yhi = lax.ppermute(yhead, 'gy', [(b, a) for a, b in up_y])  5.46 us
    pallas_call x1, Pallas kernels, fluxes(): pl.pallas_call(flux_kernel, out_shape=(jax.ShapeDtypeStruct((5, 128, 128)...  4.45 us
    ppermute x1, starting transfers between devices, local(): ylo = lax.ppermute(ytail, 'gy', up_y)  3.69 us
    ppermute x1, starting transfers between devices, local(): xhi = lax.ppermute(xhead, 'gx', [(b, a) for a, b in up_x])  2.94 us
    pallas_call x1, Pallas kernels, pack_weights(): pl.pallas_call(weight_kernel, out_shape=jax.ShapeDtypeStruct((blocks, n,...  2.47 us
    pallas_call x1, Pallas kernels, redistribute(): pl.pallas_call(mix_kernel, out_shape=jax.ShapeDtypeStruct(base.shape, F32...  2.46 us
  transfers between devices with their start and end apart: 5, of which 2 were waited for; matrix products, arithmetic and copies ran while one was open for 1% of the time, Pallas kernels for 11%

profile of v3, /device:TPU:32, one launch (start us, length us, event | category | flops | bytes accessed | tf_op | source)
XLA Modules:
  0.0 47.5 jit_solution(18259066642478078382)
XLA Ops:
  0.0 0.0 copy-start
  0.0 0.0 copy-start.1
  0.0 0.0 copy-start.3
  0.0 0.0 copy-start.4
  0.0 0.0 copy-start.2
  0.0 2.5 %weight_pack.1 = f32[32,64,128]{2,1,0:T(8,128)} custom-call(f32[32,2,64,64]{3,2,1,0:T(8,128)} %bitcast.17), custom_call_target="tpu_custom_call" | custom-call | tf_op jit(solution)/shard_map/weight_pack/pallas_call | solution.py:71
  2.5 13.2 %all-to-all-start = ((f32[32,64,128]{2,1,0:T(8,128)}), f32[32,64,128]{2,1,0:T(8,128)S(1)}, u32[]{:S(2)}, u32[]{:S(2)}) async-start(f32[32,64,128]{2,1,0:T(8,128)} %weight_pack.1), calls=%async_computation | async-start | bytes 2097152 | tf_op jit(solution)/shard_map/all_to_all | solution.py:410
  15.7 0.0 copy-done
  15.7 0.0 copy-done.1
  15.8 0.0 collective-permute-start
  15.8 2.9 %collective-permute-start.1 = (f32[5,32,128]{2,1,0:T(8,128)S(1)}, f32[5,32,128]{2,1,0:T(8,128)S(1)}, u32[]{:S(2)}, u32[]{:S(2)}) collective-permute-start(f32[5,32,128]{2,1,0:T(8,128)S(1)} %get-tuple-element.19), channel_id=1, source_target_pairs={{32,0},{64,32},{96,64},{128,96},{160,128},{192,160},{224,192},{256... | collective-permute-start | bytes 245768 | tf_op jit(solution)/shard_map/ppermute | solution.py:417
  18.7 3.7 %collective-permute-start.2 = (f32[80,128]{1,0:T(8,128)S(1)}, f32[80,128]{1,0:T(8,128)S(1)}, u32[]{:S(2)}, u32[]{:S(2)}) collective-permute-start(f32[80,128]{1,0:T(8,128)S(1)} %get-tuple-element.24), channel_id=1, source_target_pairs={{0,1},{1,2},{2,3},{3,4},{4,5},{5,6},{6,7},{7,8},{8,9},{9,10},{10,1... | collective-permute-start | bytes 122888 | tf_op jit(solution)/shard_map/ppermute | solution.py:414
  22.4 5.5 %collective-permute-start.3 = (f32[80,128]{1,0:T(8,128)S(1)}, f32[80,128]{1,0:T(8,128)S(1)}, u32[]{:S(2)}, u32[]{:S(2)}) collective-permute-start(f32[80,128]{1,0:T(8,128)S(1)} %get-tuple-element.25), channel_id=1, source_target_pairs={{1,0},{2,1},{3,2},{4,3},{5,4},{6,5},{7,6},{8,7},{9,8},{10,9},{11,1... | collective-permute-start | bytes 122888 | tf_op jit(solution)/shard_map/ppermute | solution.py:415
  27.9 0.0 copy-done.3
  27.9 0.2 convert_reduce_fusion.rank_ref
  28.7 0.0 copy-done.4
  28.7 0.1 reshape.20.cell_ref
  28.8 0.0 collective-permute-done.xlo_ref
  28.8 0.0 collective-permute-done.1.xhi_ref
  28.8 0.0 copy-done.2
  28.8 4.5 %flux_gather.1 = (f32[5,128,128]{2,1,0:T(8,128)S(1)}, f32[8,8,256]{2,1,0:T(8,128)S(1)}, f32[5,6,8,128]{3,2,1,0:T(8,128)S(1)}, f32[4,8,128]{2,1,0:T(8,128)S(1)}, ...) custom-call(s32[32]{0:T(128)S(1)} %convert_reduce_fusion.rank_ref, s32[1]{0:T(128)} %bitcast.9.live_ref, ...), custom_call_target="tpu_custom_call" | custom-call | tf_op jit(solution)/shard_map/flux_gather/pallas_call | solution.py:224
  33.3 10.8 %collective-permute-done.2.ylo_ref = f32[80,128]{1,0:T(8,128)S(1)} collective-permute-done((f32[80,128]{1,0:T(8,128)S(1)}, f32[80,128]{1,0:T(8,128)S(1)}, u32[]{:S(2)}, u32[]{:S(2)}) %collective-permute-start.2) | collective-permute-done | bytes 40992 | tf_op jit(solution)/shard_map/ppermute | solution.py:414
  44.1 0.0 collective-permute-done.3.yhi_ref
  44.1 0.5 %edge_gather.1 = (f32[5,4,8,128]{3,2,1,0:T(8,128)S(1)}, f32[8,8,256]{2,1,0:T(8,128)S(1)}, bf16[8,64,256]{2,1,0:T(8,128)(2,1)S(1)}) custom-call(s32[32,128]{1,0:T(8,128)S(1)} %get-tuple-element.20.half_ref, f32[8,256]{1,0:T(8,128)S(1)} %get-tuple-element.21.live_ref, f32[5,6,8,128]{3,2,1,0:T(8,128)S(1)} %get-tuple-element.22.edge_ref, ...), custom_call_target="tpu_custom_call" | custom-call | tf_op jit(solution)/shard_map/edge_gather/pallas_call | solution.py:314
  44.7 0.4 all-to-all-done.w_ref
  45.1 2.5 %mix_scatter.1 = f32[5,128,128]{2,1,0:T(8,128)} custom-call(s32[32]{0:T(128)S(1)} %bitcast.16, f32[32,64,128]{2,1,0:T(8,128)S(1)} %all-to-all-done.w_ref, bf16[8,64,256]{2,1,0:T(8,128)(2,1)S(1)} %get-tuple-element.27.lhs_ref, f32[8,8,256]{2,1,0:T(8,128)S(1)} %get-tuple-element.28.val_ref, s32[8,256]{1,0:T(8,128)S(1)} %reshape.20.cell_ref, ...), custom_call_target="tpu_custom_call" | custom-call | tf_op jit(solution)/shard_map/mix_scatter/pallas_call | solution.py:388
  (1 shorter events, 0.0 us)
Async XLA Ops:
  0.0 15.7 %copy-start = (f32[3,8,16,128]{3,2,1,0:T(8,128)S(1)}, f32[3,8,16,128]{3,2,1,0:T(8,128)}, u32[]{:S(2)}) copy-start(f32[3,8,16,128]{3,2,1,0:T(8,128)} %param.8) | copy-start | bytes 589828
  0.0 15.7 %copy-start.1 = (f32[2,8,16,128]{3,2,1,0:T(8,128)S(1)}, f32[2,8,16,128]{3,2,1,0:T(8,128)}, u32[]{:S(2)}) copy-start(f32[2,8,16,128]{3,2,1,0:T(8,128)} %param.7) | copy-start | bytes 393220
  0.0 27.9 %copy-start.3 = (s32[1,1,32]{2,1,0:T(1,128)S(1)}, s32[1,1,32]{2,1,0:T(1,128)}, u32[]{:S(2)}) copy-start(s32[1,1,32]{2,1,0:T(1,128)} %param.11) | copy-start | bytes 388
  0.0 28.7 %copy-start.4 = (s32[1,1,32,64]{3,2,1,0:T(8,128)S(1)}, s32[1,1,32,64]{3,2,1,0:T(8,128)}, u32[]{:S(2)}) copy-start(s32[1,1,32,64]{3,2,1,0:T(8,128)} %param.10) | copy-start | bytes 24580
  0.0 28.8 %copy-start.2 = (s32[8,16,128]{2,1,0:T(8,128)S(1)}, s32[8,16,128]{2,1,0:T(8,128)}, u32[]{:S(2)}) copy-start(s32[8,16,128]{2,1,0:T(8,128)} %param.9) | copy-start | bytes 196612
  2.5 42.6 %all-to-all-start = ((f32[32,64,128]{2,1,0:T(8,128)}), f32[32,64,128]{2,1,0:T(8,128)S(1)}, u32[]{:S(2)}, u32[]{:S(2)}) async-start(f32[32,64,128]{2,1,0:T(8,128)} %weight_pack.1), calls=%async_computation | async-start | bytes 2097152 | tf_op jit(solution)/shard_map/all_to_all | solution.py:410
  15.8 13.1 %collective-permute-start = (f32[5,32,128]{2,1,0:T(8,128)S(1)}, f32[5,32,128]{2,1,0:T(8,128)S(1)}, u32[]{:S(2)}, u32[]{:S(2)}) collective-permute-start(f32[5,32,128]{2,1,0:T(8,128)S(1)} %get-tuple-element.18), channel_id=1, source_target_pairs={{0,32},{32,64},{64,96},{96,128},{128,160},{160,192},{192,224},{224... | collective-permute-start | bytes 245768 | tf_op jit(solution)/shard_map/ppermute | solution.py:416
  15.8 13.0 %collective-permute-start.1 = (f32[5,32,128]{2,1,0:T(8,128)S(1)}, f32[5,32,128]{2,1,0:T(8,128)S(1)}, u32[]{:S(2)}, u32[]{:S(2)}) collective-permute-start(f32[5,32,128]{2,1,0:T(8,128)S(1)} %get-tuple-element.19), channel_id=1, source_target_pairs={{32,0},{64,32},{96,64},{128,96},{160,128},{192,160},{224,192},{256... | collective-permute-start | bytes 245768 | tf_op jit(solution)/shard_map/ppermute | solution.py:417
  18.7 25.4 %collective-permute-start.2 = (f32[80,128]{1,0:T(8,128)S(1)}, f32[80,128]{1,0:T(8,128)S(1)}, u32[]{:S(2)}, u32[]{:S(2)}) collective-permute-start(f32[80,128]{1,0:T(8,128)S(1)} %get-tuple-element.24), channel_id=1, source_target_pairs={{0,1},{1,2},{2,3},{3,4},{4,5},{5,6},{6,7},{7,8},{8,9},{9,10},{10,1... | collective-permute-start | bytes 122888 | tf_op jit(solution)/shard_map/ppermute | solution.py:414
  22.4 21.7 %collective-permute-start.3 = (f32[80,128]{1,0:T(8,128)S(1)}, f32[80,128]{1,0:T(8,128)S(1)}, u32[]{:S(2)}, u32[]{:S(2)}) collective-permute-start(f32[80,128]{1,0:T(8,128)S(1)} %get-tuple-element.25), channel_id=1, source_target_pairs={{1,0},{2,1},{3,2},{4,3},{5,4},{6,5},{7,6},{8,7},{9,8},{10,9},{11,1... | collective-permute-start | bytes 122888 | tf_op jit(solution)/shard_map/ppermute | solution.py:415

commit v4 on v3

--- a/solution.py
+++ b/solution.py
@@ -4,6 +4,7 @@
 from jax.experimental import pallas as pl
 from jax.experimental.pallas import tpu as pltpu
 from jax.sharding import PartitionSpec as P
+
 
 GAS_GAMMA = 1.4
 STEP_RATIO = 0.3
@@ -43,24 +44,36 @@
     )(dens_pres, velocity)
 
 
+def place_of(g):
+    x, z = g >> 3, g & 7
+    return (7 - z) * 4 + (x)
+
+
+def columns_in_order(count):
+    return sorted(range(count), key=place_of)
+
+
 def weight_kernel(w_ref, o_ref, held, packed, in_sems, out_sems):
     chunks = in_sems.shape[0]
-    step = w_ref.shape[0] // chunks
-
-    def part(c):
-        return pl.ds(c * step, step)
+    depth = w_ref.shape[1] // chunks
+    step = w_ref.shape[0] * depth
+    order = columns_in_order(chunks * step)
 
     def load(c):
-        return pltpu.make_async_copy(w_ref.at[part(c)], held.at[part(c)], in_sems.at[c])
+        part = pl.ds((chunks - 1 - c) * depth, depth)
+        return pltpu.make_async_copy(w_ref.at[:, part], held.at[:, part], in_sems.at[c])
 
     def store(c):
-        return pltpu.make_async_copy(packed.at[part(c)], o_ref.at[part(c)], out_sems.at[c])
+        part = pl.ds(c * step, step)
+        return pltpu.make_async_copy(packed.at[part], o_ref.at[part], out_sems.at[c])
 
     for c in range(chunks):
         load(c).start()
     for c in range(chunks):
         load(c).wait()
-        packed[part(c)] = jnp.concatenate([held[part(c), 0], held[part(c), 1]], axis=-1)
+        for k in range(c * step, (c + 1) * step):
+            x, z = order[k] >> 3, order[k] & 7
+            packed[k] = jnp.concatenate([held[x, z, 0], held[x, z, 1]], axis=-1)
         store(c).start()
     for c in range(chunks):
         store(c).wait()
@@ -68,6 +81,7 @@
 
 def pack_weights(weights):
     blocks, cap, n, _ = weights.shape
+    weights = weights.reshape(4, 8, cap, n, n)
     return pl.pallas_call(
         weight_kernel,
         out_shape=jax.ShapeDtypeStruct((blocks, n, cap * n), F32),
@@ -346,7 +360,7 @@
     for q in range(8):
         tiles = []
         for t in range(4):
-            w_hi, w_lo = two_parts(w_ref[helper[q * 4 + t]])
+            w_hi, w_lo = two_parts(w_ref[place_of(helper[q * 4 + t])])
             tiles.append(jnp.concatenate([w_hi, w_lo], axis=1))
         got = contract_last(lhs_ref[q], jnp.concatenate(tiles, axis=0))
         got = got[0:32] + got[32:64]
@@ -407,7 +421,14 @@
     velocity = velocity.reshape(3, 128, 128)
     cut_class = cut_class.reshape(128, 128)
     packed = pack_weights(redist_weights[0, 0])
-    weights = lax.all_to_all(packed, "gy", split_axis=0, concat_axis=0, tiled=True)
+    weights = lax.all_to_all(
+        packed,
+        "gy",
+        split_axis=0,
+        concat_axis=0,
+        axis_index_groups=[columns_in_order(ngy)],
+        tiled=True,
+    )
     xhead, xtail, yhead, ytail = pack_halo(dens_pres, velocity)
     up_x = [(i, (i + 1) % ngx) for i in range(ngx)]
     up_y = [(i, (i + 1) % ngy) for i in range(ngy)]

time: 47.8 us -> 44.8 us (0.937)
  the two profiles are of different devices: /device:TPU:32 before, /device:TPU:40 now
where the time goes in v4:
time: 44.8 us; the launch traced here: 44.5 us
  starting transfers between devices  24.5 us (55%)
  Pallas kernels  9.97 us (22%)
  waiting for transfers between devices  8.99 us (20%)
  between operations  0.78 us (2%)
    all_to_all x1, starting transfers between devices, local(): lax.all_to_all(packed, 'gy', split_axis=0, concat_axis=0, axis_index_grou...  13.6 us
    ppermute x1, waiting for transfers between devices, local(): ylo = lax.ppermute(ytail, 'gy', up_y)  8.84 us
    ppermute x1, starting transfers between devices, local(): yhi = lax.ppermute(yhead, 'gy', [(b, a) for a, b in up_y])  5.82 us
    pallas_call x1, Pallas kernels, fluxes(): pl.pallas_call(flux_kernel, out_shape=(jax.ShapeDtypeStruct((5, 128, 128)...  4.45 us
    ppermute x1, starting transfers between devices, local(): ylo = lax.ppermute(ytail, 'gy', up_y)  3.33 us
    pallas_call x1, Pallas kernels, redistribute(): pl.pallas_call(mix_kernel, out_shape=jax.ShapeDtypeStruct(base.shape, F32...  2.47 us
    pallas_call x1, Pallas kernels, pack_weights(): pl.pallas_call(weight_kernel, out_shape=jax.ShapeDtypeStruct((blocks, n,...  2.47 us
    ppermute x1, starting transfers between devices, local(): xhi = lax.ppermute(xhead, 'gx', [(b, a) for a, b in up_x])  1.73 us
  transfers between devices with their start and end apart: 5, of which 2 were waited for; matrix products, arithmetic and copies ran while one was open for 1% of the time, Pallas kernels for 11%

profile of v4, /device:TPU:40, one launch (start us, length us, event | category | flops | bytes accessed | tf_op | source)
XLA Modules:
  0.0 44.5 jit_solution(13990549317383399905)
XLA Ops:
  0.0 0.0 copy-start
  0.0 0.0 copy-start.1
  0.0 0.0 copy-start.3
  0.0 0.0 copy-start.4
  0.0 0.0 copy-start.2
  0.0 2.5 %weight_pack.1 = f32[32,64,128]{2,1,0:T(8,128)} custom-call(f32[4,8,2,64,64]{4,3,2,1,0:T(8,128)} %bitcast.17), custom_call_target="tpu_custom_call" | custom-call | tf_op jit(solution)/shard_map/weight_pack/pallas_call | solution.py:85
  2.5 13.6 %all-to-all-start = ((f32[32,64,128]{2,1,0:T(8,128)}), f32[32,64,128]{2,1,0:T(8,128)S(1)}, u32[]{:S(2)}, u32[]{:S(2)}) async-start(f32[32,64,128]{2,1,0:T(8,128)} %weight_pack.1), calls=%async_computation | async-start | bytes 2097152 | tf_op jit(solution)/shard_map/all_to_all | solution.py:424
  16.1 0.0 copy-done
  16.1 0.0 copy-done.1
  16.2 0.0 collective-permute-start
  16.2 1.7 %collective-permute-start.1 = (f32[5,32,128]{2,1,0:T(8,128)S(1)}, f32[5,32,128]{2,1,0:T(8,128)S(1)}, u32[]{:S(2)}, u32[]{:S(2)}) collective-permute-start(f32[5,32,128]{2,1,0:T(8,128)S(1)} %get-tuple-element.19), channel_id=1, source_target_pairs={{32,0},{64,32},{96,64},{128,96},{160,128},{192,160},{224,192},{256... | collective-permute-start | bytes 245768 | tf_op jit(solution)/shard_map/ppermute | solution.py:438
  17.9 3.3 %collective-permute-start.2 = (f32[80,128]{1,0:T(8,128)S(1)}, f32[80,128]{1,0:T(8,128)S(1)}, u32[]{:S(2)}, u32[]{:S(2)}) collective-permute-start(f32[80,128]{1,0:T(8,128)S(1)} %get-tuple-element.24), channel_id=1, source_target_pairs={{0,1},{1,2},{2,3},{3,4},{4,5},{5,6},{6,7},{7,8},{8,9},{9,10},{10,1... | collective-permute-start | bytes 122888 | tf_op jit(solution)/shard_map/ppermute | solution.py:435
  21.2 5.8 %collective-permute-start.3 = (f32[80,128]{1,0:T(8,128)S(1)}, f32[80,128]{1,0:T(8,128)S(1)}, u32[]{:S(2)}, u32[]{:S(2)}) collective-permute-start(f32[80,128]{1,0:T(8,128)S(1)} %get-tuple-element.25), channel_id=1, source_target_pairs={{1,0},{2,1},{3,2},{4,3},{5,4},{6,5},{7,6},{8,7},{9,8},{10,9},{11,1... | collective-permute-start | bytes 122888 | tf_op jit(solution)/shard_map/ppermute | solution.py:436
  27.1 0.0 copy-done.3
  27.1 0.2 convert_reduce_fusion.rank_ref
  27.9 0.0 copy-done.4
  27.9 0.1 reshape.20.cell_ref
  28.0 0.0 collective-permute-done.xlo_ref
  28.0 0.0 collective-permute-done.1.xhi_ref
  28.0 0.0 copy-done.2
  28.0 4.5 %flux_gather.1 = (f32[5,128,128]{2,1,0:T(8,128)S(1)}, f32[8,8,256]{2,1,0:T(8,128)S(1)}, f32[5,6,8,128]{3,2,1,0:T(8,128)S(1)}, f32[4,8,128]{2,1,0:T(8,128)S(1)}, ...) custom-call(s32[32]{0:T(128)S(1)} %convert_reduce_fusion.rank_ref, s32[1]{0:T(128)} %bitcast.9.live_ref, ...), custom_call_target="tpu_custom_call" | custom-call | tf_op jit(solution)/shard_map/flux_gather/pallas_call | solution.py:238
  32.5 8.8 %collective-permute-done.2.ylo_ref = f32[80,128]{1,0:T(8,128)S(1)} collective-permute-done((f32[80,128]{1,0:T(8,128)S(1)}, f32[80,128]{1,0:T(8,128)S(1)}, u32[]{:S(2)}, u32[]{:S(2)}) %collective-permute-start.2) | collective-permute-done | bytes 40992 | tf_op jit(solution)/shard_map/ppermute | solution.py:435
  41.3 0.0 collective-permute-done.3.yhi_ref
  41.3 0.5 %edge_gather.1 = (f32[5,4,8,128]{3,2,1,0:T(8,128)S(1)}, f32[8,8,256]{2,1,0:T(8,128)S(1)}, bf16[8,64,256]{2,1,0:T(8,128)(2,1)S(1)}) custom-call(s32[32,128]{1,0:T(8,128)S(1)} %get-tuple-element.20.half_ref, f32[8,256]{1,0:T(8,128)S(1)} %get-tuple-element.21.live_ref, f32[5,6,8,128]{3,2,1,0:T(8,128)S(1)} %get-tuple-element.22.edge_ref, ...), custom_call_target="tpu_custom_call" | custom-call | tf_op jit(solution)/shard_map/edge_gather/pallas_call | solution.py:328
  41.9 0.1 all-to-all-done.w_ref
  42.0 2.5 %mix_scatter.1 = f32[5,128,128]{2,1,0:T(8,128)} custom-call(s32[32]{0:T(128)S(1)} %bitcast.16, f32[32,64,128]{2,1,0:T(8,128)S(1)} %all-to-all-done.w_ref, bf16[8,64,256]{2,1,0:T(8,128)(2,1)S(1)} %get-tuple-element.27.lhs_ref, f32[8,8,256]{2,1,0:T(8,128)S(1)} %get-tuple-element.28.val_ref, s32[8,256]{1,0:T(8,128)S(1)} %reshape.20.cell_ref, ...), custom_call_target="tpu_custom_call" | custom-call | tf_op jit(solution)/shard_map/mix_scatter/pallas_call | solution.py:402
  (1 shorter events, 0.0 us)
Async XLA Ops:
  0.0 16.1 %copy-start = (f32[3,8,16,128]{3,2,1,0:T(8,128)S(1)}, f32[3,8,16,128]{3,2,1,0:T(8,128)}, u32[]{:S(2)}) copy-start(f32[3,8,16,128]{3,2,1,0:T(8,128)} %param.8) | copy-start | bytes 589828
  0.0 16.1 %copy-start.1 = (f32[2,8,16,128]{3,2,1,0:T(8,128)S(1)}, f32[2,8,16,128]{3,2,1,0:T(8,128)}, u32[]{:S(2)}) copy-start(f32[2,8,16,128]{3,2,1,0:T(8,128)} %param.7) | copy-start | bytes 393220
  0.0 27.1 %copy-start.3 = (s32[1,1,32]{2,1,0:T(1,128)S(1)}, s32[1,1,32]{2,1,0:T(1,128)}, u32[]{:S(2)}) copy-start(s32[1,1,32]{2,1,0:T(1,128)} %param.11) | copy-start | bytes 388
  0.0 27.9 %copy-start.4 = (s32[1,1,32,64]{3,2,1,0:T(8,128)S(1)}, s32[1,1,32,64]{3,2,1,0:T(8,128)}, u32[]{:S(2)}) copy-start(s32[1,1,32,64]{3,2,1,0:T(8,128)} %param.10) | copy-start | bytes 24580
  0.0 28.0 %copy-start.2 = (s32[8,16,128]{2,1,0:T(8,128)S(1)}, s32[8,16,128]{2,1,0:T(8,128)}, u32[]{:S(2)}) copy-start(s32[8,16,128]{2,1,0:T(8,128)} %param.9) | copy-start | bytes 196612
  2.5 39.5 %all-to-all-start = ((f32[32,64,128]{2,1,0:T(8,128)}), f32[32,64,128]{2,1,0:T(8,128)S(1)}, u32[]{:S(2)}, u32[]{:S(2)}) async-start(f32[32,64,128]{2,1,0:T(8,128)} %weight_pack.1), calls=%async_computation | async-start | bytes 2097152 | tf_op jit(solution)/shard_map/all_to_all | solution.py:424
  16.2 11.9 %collective-permute-start = (f32[5,32,128]{2,1,0:T(8,128)S(1)}, f32[5,32,128]{2,1,0:T(8,128)S(1)}, u32[]{:S(2)}, u32[]{:S(2)}) collective-permute-start(f32[5,32,128]{2,1,0:T(8,128)S(1)} %get-tuple-element.18), channel_id=1, source_target_pairs={{0,32},{32,64},{64,96},{96,128},{128,160},{160,192},{192,224},{224... | collective-permute-start | bytes 245768 | tf_op jit(solution)/shard_map/ppermute | solution.py:437
  16.2 11.8 %collective-permute-start.1 = (f32[5,32,128]{2,1,0:T(8,128)S(1)}, f32[5,32,128]{2,1,0:T(8,128)S(1)}, u32[]{:S(2)}, u32[]{:S(2)}) collective-permute-start(f32[5,32,128]{2,1,0:T(8,128)S(1)} %get-tuple-element.19), channel_id=1, source_target_pairs={{32,0},{64,32},{96,64},{128,96},{160,128},{192,160},{224,192},{256... | collective-permute-start | bytes 245768 | tf_op jit(solution)/shard_map/ppermute | solution.py:438
  17.9 23.4 %collective-permute-start.2 = (f32[80,128]{1,0:T(8,128)S(1)}, f32[80,128]{1,0:T(8,128)S(1)}, u32[]{:S(2)}, u32[]{:S(2)}) collective-permute-start(f32[80,128]{1,0:T(8,128)S(1)} %get-tuple-element.24), channel_id=1, source_target_pairs={{0,1},{1,2},{2,3},{3,4},{4,5},{5,6},{6,7},{7,8},{8,9},{9,10},{10,1... | collective-permute-start | bytes 122888 | tf_op jit(solution)/shard_map/ppermute | solution.py:435
  21.2 20.1 %collective-permute-start.3 = (f32[80,128]{1,0:T(8,128)S(1)}, f32[80,128]{1,0:T(8,128)S(1)}, u32[]{:S(2)}, u32[]{:S(2)}) collective-permute-start(f32[80,128]{1,0:T(8,128)S(1)} %get-tuple-element.25), channel_id=1, source_target_pairs={{1,0},{2,1},{3,2},{4,3},{5,4},{6,5},{7,6},{8,7},{9,8},{10,9},{11,1... | collective-permute-start | bytes 122888 | tf_op jit(solution)/shard_map/ppermute | solution.py:436

commit v5 on v4

--- a/solution.py
+++ b/solution.py
@@ -4,7 +4,6 @@
 from jax.experimental import pallas as pl
 from jax.experimental.pallas import tpu as pltpu
 from jax.sharding import PartitionSpec as P
-
 
 GAS_GAMMA = 1.4
 STEP_RATIO = 0.3
@@ -253,10 +252,7 @@
     )(ranks, live, dens_pres, velocity, cut_class, xlo, xhi, cells)
 
 
-def edge_kernel(
-    half_ref, live_ref, edge_ref, scale_ref, ylo_ref, yhi_ref, cell_ref, part_ref,
-    fix_ref, val_ref, lhs_ref,
-):
+def edge_values(half_ref, live_ref, edge_ref, scale_ref, ylo_ref, yhi_ref, cell_ref, part_ref):
     def halo(ref, j):
         return [ref[c * 16 + j * 8 : c * 16 + j * 8 + 8, :] for c in range(5)]
 
@@ -286,8 +282,6 @@
                 scale_ref[3] * (face_d[c] - face_c[c]),
             ]
         )
-        for j in range(4):
-            fix_ref[c, j] = fix[c][j]
     table = jnp.concatenate(
         [
             jnp.concatenate([fix[c][j], fix[c][j + 2]], axis=1)
@@ -298,13 +292,15 @@
     )
     pieces = jnp.concatenate(two_parts(table), axis=0)
     half_id = lax.broadcasted_iota(jnp.int32, (8, 128), 1) // 64
+    vals, operands, lane_hots = [], [], []
     for q in range(8):
         cell = cell_ref[q : q + 1, :]
         x, y, z = cell >> 11, (cell >> 7) & 15, cell & 127
         on_edge = (y < 2) | (y > 13)
         row = jnp.where(on_edge, (y & 1) * 8 + x, -1)
         lane = (y >> 3) * 128 + z
-        got = jnp.dot(pieces, one_hot(lane, 256).astype(F32).astype(BF16), preferred_element_type=F32)
+        lane_hots.append(one_hot(lane, 256).astype(F32).astype(BF16))
+        got = jnp.dot(pieces, lane_hots[q], preferred_element_type=F32)
         got = got[0:80] + got[80:160]
         row_hot = one_hot(row, 16)
         rows = [
@@ -313,7 +309,7 @@
         ]
         val = part_ref[q] + jnp.concatenate(rows + [jnp.zeros((3, 256), F32)], axis=0)
         val = jnp.where(live_ref[q : q + 1, :] > 0.0, val, 0.0)
-        val_ref[q] = val
+        vals.append(val)
         placed = []
         for t in range(4):
             piece = val[:, (t // 2) * 128 : (t // 2) * 128 + 128]
@@ -321,22 +317,8 @@
             moved = jnp.where(rank == t % 2, piece, pltpu.roll(piece, 64, 1))
             placed.append(jnp.where(half_id == rank, moved, 0.0))
         both = jnp.concatenate(two_parts(jnp.concatenate(placed, axis=0)), axis=0)
-        lhs_ref[q] = jnp.concatenate([both, both], axis=1)
-
-
-def edges(half, live, edge, scale, ylo, yhi, cells, part):
-    return pl.pallas_call(
-        edge_kernel,
-        out_shape=(
-            jax.ShapeDtypeStruct((5, 4, 8, 128), F32),
-            jax.ShapeDtypeStruct((8, 8, 256), F32),
-            jax.ShapeDtypeStruct((8, 64, 256), BF16),
-        ),
-        in_specs=[VMEM_SPEC] * 8,
-        out_specs=(VMEM_SPEC,) * 3,
-        compiler_params=PARAMS,
-        name="edge_gather",
-    )(half, live, edge, scale, ylo, yhi, cells, part)
+        operands.append(jnp.concatenate([both, both], axis=1))
+    return fix, vals, operands, lane_hots
 
 
 def contract_last(a, b):
@@ -344,17 +326,16 @@
 
 
 def mix_kernel(
-    helper_ref, w_ref, lhs_ref, val_ref, cell_ref, base_ref, fix_ref, out_ref,
-    helper, made, helper_sem, out_sems,
+    helper_ref, w_ref, half_ref, live_ref, edge_ref, scale_ref, ylo_ref, yhi_ref, cell_ref, part_ref,
+    base_ref, out_ref, helper, made, helper_sem, out_sems,
 ):
     fetch = pltpu.make_async_copy(helper_ref, helper, helper_sem)
     fetch.start()
+    fix, vals, operands, lane_hots = edge_values(
+        half_ref, live_ref, edge_ref, scale_ref, ylo_ref, yhi_ref, cell_ref, part_ref
+    )
     slot_of = lax.broadcasted_iota(jnp.int32, (8, 256), 1) // 64
-    lane_hots, row_hots = [], []
-    for q in range(8):
-        row, lane = cell_parts(cell_ref[q : q + 1, :])
-        row_hots.append(one_hot(row, 64))
-        lane_hots.append(one_hot(lane, 256).astype(F32).astype(BF16))
+    row_hots = [one_hot(cell_parts(cell_ref[q : q + 1, :])[0], 64) for q in range(8)]
     fetch.wait()
     diffs = []
     for q in range(8):
@@ -362,12 +343,12 @@
         for t in range(4):
             w_hi, w_lo = two_parts(w_ref[place_of(helper[q * 4 + t])])
             tiles.append(jnp.concatenate([w_hi, w_lo], axis=1))
-        got = contract_last(lhs_ref[q], jnp.concatenate(tiles, axis=0))
+        got = contract_last(operands[q], jnp.concatenate(tiles, axis=0))
         got = got[0:32] + got[32:64]
         mixed = got[0:8]
         for t in range(1, 4):
             mixed = jnp.where(slot_of == t, got[t * 8 : t * 8 + 8], mixed)
-        diffs.append(mixed - val_ref[q])
+        diffs.append(mixed - vals[q])
     columns = []
     for q in range(8):
         d_hi = diffs[q].astype(BF16).astype(F32)
@@ -392,17 +373,17 @@
             made[v, bottom, :] = base_ref[v, bottom, :] + total[row : row + 8, 128:256]
         for j, y in enumerate((0, 1, 14, 15)):
             rows = pl.ds(y, 8, stride=16)
-            made[v, rows, :] = made[v, rows, :] + fix_ref[v, j]
+            made[v, rows, :] = made[v, rows, :] + fix[v][j]
         store(v).start()
     for v in range(5):
         store(v).wait()
 
 
-def redistribute(helpers, weights, lhs, val, cells, base, fix):
+def redistribute(helpers, weights, half, live, edge, scale, ylo, yhi, cells, part, base):
     return pl.pallas_call(
         mix_kernel,
         out_shape=jax.ShapeDtypeStruct(base.shape, F32),
-        in_specs=[ANY_SPEC] + [VMEM_SPEC] * 6,
+        in_specs=[ANY_SPEC] + [VMEM_SPEC] * 10,
         out_specs=ANY_SPEC,
         scratch_shapes=[
             pltpu.SMEM((32,), jnp.int32),
@@ -412,7 +393,7 @@
         ],
         compiler_params=PARAMS,
         name="mix_scatter",
-    )(helpers, weights, lhs, val, cells, base, fix)
+    )(helpers, weights, half, live, edge, scale, ylo, yhi, cells, part, base)
 
 
 def local(dens_pres, velocity, cut_class, nbhd_cells, helper_list, live_counts, redist_weights):
@@ -447,8 +428,9 @@
     base, part, edge, scale, half, live = fluxes(
         ranks, live_counts[0], dens_pres, velocity, cut_class, xlo, xhi, cells
     )
-    fix, val, lhs = edges(half, live, edge, scale, ylo, yhi, cells, part)
-    out = redistribute(helpers, weights, lhs, val, cells, base, fix)
+    out = redistribute(
+        helpers, weights, half, live, edge, scale, ylo, yhi, cells, part, base
+    )
     return out.reshape(5, 8, 16, 128)
 
 

time: 44.8 us -> 45 us (level)
  the two profiles are of different devices: /device:TPU:40 before, /device:TPU:8 now
where the time goes in v5:
time: 45 us; the launch traced here: 44.7 us
  starting transfers between devices  24.5 us (54%)
  Pallas kernels  9.64 us (21%)
  waiting for transfers between devices  9.54 us (21%)
  between operations  0.77 us (2%)
    all_to_all x1, starting transfers between devices, local(): lax.all_to_all(packed, 'gy', split_axis=0, concat_axis=0, axis_index_grou...  13.6 us
    ppermute x1, waiting for transfers between devices, local(): ylo = lax.ppermute(ytail, 'gy', up_y)  8.84 us
    ppermute x1, starting transfers between devices, local(): yhi = lax.ppermute(yhead, 'gy', [(b, a) for a, b in up_y])  5.82 us
    pallas_call x1, Pallas kernels, fluxes(): pl.pallas_call(flux_kernel, out_shape=(jax.ShapeDtypeStruct((5, 128, 128)...  4.46 us
    ppermute x1, starting transfers between devices, local(): ylo = lax.ppermute(ytail, 'gy', up_y)  3.33 us
    pallas_call x1, Pallas kernels, redistribute(): pl.pallas_call(mix_kernel, out_shape=jax.ShapeDtypeStruct(base.shape, F32...  2.68 us
    pallas_call x1, Pallas kernels, pack_weights(): pl.pallas_call(weight_kernel, out_shape=jax.ShapeDtypeStruct((blocks, n,...  2.46 us
    ppermute x1, starting transfers between devices, local(): xhi = lax.ppermute(xhead, 'gx', [(b, a) for a, b in up_x])  1.73 us
  transfers between devices with their start and end apart: 5, of which 2 were waited for; matrix products, arithmetic and copies ran while one was open for 1% of the time, Pallas kernels for 10%

profile of v5, /device:TPU:8, one launch (start us, length us, event | category | flops | bytes accessed | tf_op | source)
XLA Modules:
  0.0 44.7 jit_solution(13650542768568244402)
XLA Ops:
  0.0 0.0 copy-start
  0.0 0.0 copy-start.1
  0.0 0.0 copy-start.3
  0.0 0.0 copy-start.4
  0.0 0.0 copy-start.2
  0.0 2.5 %weight_pack.1 = f32[32,64,128]{2,1,0:T(8,128)} custom-call(f32[4,8,2,64,64]{4,3,2,1,0:T(8,128)} %bitcast.17), custom_call_target="tpu_custom_call" | custom-call | tf_op jit(solution)/shard_map/weight_pack/pallas_call | solution.py:84
  2.5 13.6 %all-to-all-start = ((f32[32,64,128]{2,1,0:T(8,128)}), f32[32,64,128]{2,1,0:T(8,128)S(1)}, u32[]{:S(2)}, u32[]{:S(2)}) async-start(f32[32,64,128]{2,1,0:T(8,128)} %weight_pack.1), calls=%async_computation | async-start | bytes 2097152 | tf_op jit(solution)/shard_map/all_to_all | solution.py:405
  16.1 0.0 copy-done
  16.1 0.0 copy-done.1
  16.1 0.0 collective-permute-start
  16.2 1.7 %collective-permute-start.1 = (f32[5,32,128]{2,1,0:T(8,128)S(1)}, f32[5,32,128]{2,1,0:T(8,128)S(1)}, u32[]{:S(2)}, u32[]{:S(2)}) collective-permute-start(f32[5,32,128]{2,1,0:T(8,128)S(1)} %get-tuple-element.16), channel_id=1, source_target_pairs={{32,0},{64,32},{96,64},{128,96},{160,128},{192,160},{224,192},{256... | collective-permute-start | bytes 245768 | tf_op jit(solution)/shard_map/ppermute | solution.py:419
  17.9 3.3 %collective-permute-start.2 = (f32[80,128]{1,0:T(8,128)S(1)}, f32[80,128]{1,0:T(8,128)S(1)}, u32[]{:S(2)}, u32[]{:S(2)}) collective-permute-start(f32[80,128]{1,0:T(8,128)S(1)} %get-tuple-element.21), channel_id=1, source_target_pairs={{0,1},{1,2},{2,3},{3,4},{4,5},{5,6},{6,7},{7,8},{8,9},{9,10},{10,1... | collective-permute-start | bytes 122888 | tf_op jit(solution)/shard_map/ppermute | solution.py:416
  21.2 5.8 %collective-permute-start.3 = (f32[80,128]{1,0:T(8,128)S(1)}, f32[80,128]{1,0:T(8,128)S(1)}, u32[]{:S(2)}, u32[]{:S(2)}) collective-permute-start(f32[80,128]{1,0:T(8,128)S(1)} %get-tuple-element.22), channel_id=1, source_target_pairs={{1,0},{2,1},{3,2},{4,3},{5,4},{6,5},{7,6},{8,7},{9,8},{10,9},{11,1... | collective-permute-start | bytes 122888 | tf_op jit(solution)/shard_map/ppermute | solution.py:417
  27.1 0.0 copy-done.3
  27.1 0.2 convert_reduce_fusion.rank_ref
  27.9 0.0 copy-done.4
  27.9 0.1 reshape.20.cell_ref
  28.0 0.0 collective-permute-done.xlo_ref
  28.0 0.0 collective-permute-done.1.xhi_ref
  28.0 0.0 copy-done.2
  28.0 4.5 %flux_gather.1 = (f32[5,128,128]{2,1,0:T(8,128)S(1)}, f32[8,8,256]{2,1,0:T(8,128)S(1)}, f32[5,6,8,128]{3,2,1,0:T(8,128)S(1)}, f32[4,8,128]{2,1,0:T(8,128)S(1)}, ...) custom-call(s32[32]{0:T(128)S(1)} %convert_reduce_fusion.rank_ref, s32[1]{0:T(128)} %bitcast.9.live_ref, ...), custom_call_target="tpu_custom_call" | custom-call | tf_op jit(solution)/shard_map/flux_gather/pallas_call | solution.py:237
  32.5 8.8 %collective-permute-done.2.ylo_ref = f32[80,128]{1,0:T(8,128)S(1)} collective-permute-done((f32[80,128]{1,0:T(8,128)S(1)}, f32[80,128]{1,0:T(8,128)S(1)}, u32[]{:S(2)}, u32[]{:S(2)}) %collective-permute-start.2) | collective-permute-done | bytes 40992 | tf_op jit(solution)/shard_map/ppermute | solution.py:416
  41.3 0.0 collective-permute-done.3.yhi_ref
  41.3 0.7 %all-to-all-done.w_ref = f32[32,64,128]{2,1,0:T(8,128)S(1)} async-done(((f32[32,64,128]{2,1,0:T(8,128)}), f32[32,64,128]{2,1,0:T(8,128)S(1)}, u32[]{:S(2)}, u32[]{:S(2)}) %all-to-all-start) | async-done | bytes 1048608 | tf_op jit(solution)/shard_map/all_to_all | solution.py:405
  42.0 2.7 %mix_scatter.1 = f32[5,128,128]{2,1,0:T(8,128)} custom-call(s32[32]{0:T(128)S(1)} %bitcast.16, f32[32,64,128]{2,1,0:T(8,128)S(1)} %all-to-all-done.w_ref, s32[32,128]{1,0:T(8,128)S(1)} %get-tuple-element.17.half_ref, f32[8,256]{1,0:T(8,128)S(1)} %get-tuple-element.18.live_ref, f32[5,6,8,128]{3,2,1,0:T(8,128)S(1)} %get-tuple-element.19.edge_ref, ...), custom_call_target="tpu_custom_call" | custom-call | tf_op jit(solution)/shard_map/mix_scatter/pallas_call | solution.py:383
  (1 shorter events, 0.0 us)
Async XLA Ops:
  0.0 16.1 %copy-start = (f32[3,8,16,128]{3,2,1,0:T(8,128)S(1)}, f32[3,8,16,128]{3,2,1,0:T(8,128)}, u32[]{:S(2)}) copy-start(f32[3,8,16,128]{3,2,1,0:T(8,128)} %param.8) | copy-start | bytes 589828
  0.0 16.1 %copy-start.1 = (f32[2,8,16,128]{3,2,1,0:T(8,128)S(1)}, f32[2,8,16,128]{3,2,1,0:T(8,128)}, u32[]{:S(2)}) copy-start(f32[2,8,16,128]{3,2,1,0:T(8,128)} %param.7) | copy-start | bytes 393220
  0.0 27.1 %copy-start.3 = (s32[1,1,32]{2,1,0:T(1,128)S(1)}, s32[1,1,32]{2,1,0:T(1,128)}, u32[]{:S(2)}) copy-start(s32[1,1,32]{2,1,0:T(1,128)} %param.11) | copy-start | bytes 388
  0.0 27.9 %copy-start.4 = (s32[1,1,32,64]{3,2,1,0:T(8,128)S(1)}, s32[1,1,32,64]{3,2,1,0:T(8,128)}, u32[]{:S(2)}) copy-start(s32[1,1,32,64]{3,2,1,0:T(8,128)} %param.10) | copy-start | bytes 24580
  0.0 28.0 %copy-start.2 = (s32[8,16,128]{2,1,0:T(8,128)S(1)}, s32[8,16,128]{2,1,0:T(8,128)}, u32[]{:S(2)}) copy-start(s32[8,16,128]{2,1,0:T(8,128)} %param.9) | copy-start | bytes 196612
  2.5 39.5 %all-to-all-start = ((f32[32,64,128]{2,1,0:T(8,128)}), f32[32,64,128]{2,1,0:T(8,128)S(1)}, u32[]{:S(2)}, u32[]{:S(2)}) async-start(f32[32,64,128]{2,1,0:T(8,128)} %weight_pack.1), calls=%async_computation | async-start | bytes 2097152 | tf_op jit(solution)/shard_map/all_to_all | solution.py:405
  16.1 11.9 %collective-permute-start = (f32[5,32,128]{2,1,0:T(8,128)S(1)}, f32[5,32,128]{2,1,0:T(8,128)S(1)}, u32[]{:S(2)}, u32[]{:S(2)}) collective-permute-start(f32[5,32,128]{2,1,0:T(8,128)S(1)} %get-tuple-element.15), channel_id=1, source_target_pairs={{0,32},{32,64},{64,96},{96,128},{128,160},{160,192},{192,224},{224... | collective-permute-start | bytes 245768 | tf_op jit(solution)/shard_map/ppermute | solution.py:418
  16.2 11.8 %collective-permute-start.1 = (f32[5,32,128]{2,1,0:T(8,128)S(1)}, f32[5,32,128]{2,1,0:T(8,128)S(1)}, u32[]{:S(2)}, u32[]{:S(2)}) collective-permute-start(f32[5,32,128]{2,1,0:T(8,128)S(1)} %get-tuple-element.16), channel_id=1, source_target_pairs={{32,0},{64,32},{96,64},{128,96},{160,128},{192,160},{224,192},{256... | collective-permute-start | bytes 245768 | tf_op jit(solution)/shard_map/ppermute | solution.py:419
  17.9 23.4 %collective-permute-start.2 = (f32[80,128]{1,0:T(8,128)S(1)}, f32[80,128]{1,0:T(8,128)S(1)}, u32[]{:S(2)}, u32[]{:S(2)}) collective-permute-start(f32[80,128]{1,0:T(8,128)S(1)} %get-tuple-element.21), channel_id=1, source_target_pairs={{0,1},{1,2},{2,3},{3,4},{4,5},{5,6},{6,7},{7,8},{8,9},{9,10},{10,1... | collective-permute-start | bytes 122888 | tf_op jit(solution)/shard_map/ppermute | solution.py:416
  21.2 20.1 %collective-permute-start.3 = (f32[80,128]{1,0:T(8,128)S(1)}, f32[80,128]{1,0:T(8,128)S(1)}, u32[]{:S(2)}, u32[]{:S(2)}) collective-permute-start(f32[80,128]{1,0:T(8,128)S(1)} %get-tuple-element.22), channel_id=1, source_target_pairs={{1,0},{2,1},{3,2},{4,3},{5,4},{6,5},{7,6},{8,7},{9,8},{10,9},{11,1... | collective-permute-start | bytes 122888 | tf_op jit(solution)/shard_map/ppermute | solution.py:417
